TPU v7x, 256 devices: a whole 4x4x8 slice. The times are simulated.
256 devices in a mesh: grp: 4 (over z_hi), col: 16 (over y, z_lo, core), lay: 4 (over x).
Axes of the slice: x: 4, y: 4, z: 8 (z_hi: 4, z_lo: 2; z = z_hi * 2 + z_lo), core: 2. Of those that a mesh axis runs over, the one named last changes fastest.
Arguments:
- salinity: float32 [16, 1024, 2048], P('lay', ('grp', 'col')), may hold values from 0.3 to 4.2
- zone_ids: int32 [16, 1024, 2048], P('lay', ('grp', 'col')), may hold values from 0 to 7
- flow_speed: float32 [16, 1024, 2048], P('lay', ('grp', 'col')), may hold values from 0.5 to 4
- fixed_cells: int32 [16, 1024, 2048], P('lay', ('grp', 'col')), may hold values 0 or 1
- dispersivity: float32 [2, 8], replicated, may hold values from 50 to 1000
Outputs:
- salinity_next: float32 [16, 1024, 2048], P('lay', 'grp', 'col')
All inputs are finite; a program needn't handle non-finite values. No bound on the sum of `fixed_cells` on one device may be relied on, other than what follows from the above.
Results may differ from a plain program's by a relative error of at most 0.00005.
Values sent between devices are 32-bit elements; how exact they have to be, the bound alone decides.
A program may use at most 128 MiB of HBM per device.

v0:
```python
import jax
import jax.numpy as jnp
from jax import lax
from jax.sharding import PartitionSpec as P


def shifted(values, stride, line_axis, filler, heading):
    line_axis = line_axis % values.ndim
    length = values.shape[line_axis]
    edge_shape = list(values.shape)
    edge_shape[line_axis] = length
    padding = jnp.full(tuple(edge_shape), filler, values.dtype)
    padded = jnp.concatenate([padding, values, padding], axis=line_axis)
    return lax.dynamic_slice_in_dim(padded, length + heading * stride, length, axis=line_axis)


def reduce_lines(below_coef, middle, above_coef, right_side, line_axis):
    length = middle.shape[line_axis]
    levels = max(1, (length - 1).bit_length())

    def one_level(_, carry):
        below_now, middle_now, above_now, right_now, stride = carry
        weight_below = -below_now / shifted(middle_now, stride, line_axis, 1.0, -1)
        weight_above = -above_now / shifted(middle_now, stride, line_axis, 1.0, 1)
        below_next = weight_below * shifted(below_now, stride, line_axis, 0.0, -1)
        above_next = weight_above * shifted(above_now, stride, line_axis, 0.0, 1)
        middle_next = (
            middle_now
            + weight_below * shifted(above_now, stride, line_axis, 0.0, -1)
            + weight_above * shifted(below_now, stride, line_axis, 0.0, 1)
        )
        right_next = (
            right_now
            + weight_below * shifted(right_now, stride, line_axis, 0.0, -1)
            + weight_above * shifted(right_now, stride, line_axis, 0.0, 1)
        )
        return (below_next, middle_next, above_next, right_next, stride * 2)

    result = lax.fori_loop(
        0, levels, one_level, (below_coef, middle, above_coef, right_side, jnp.int32(1))
    )
    return result[3] / result[1]


def line_solve(coupling, field, line_axis):
    return reduce_lines(-coupling, 1.0 + 2.0 * coupling, -coupling, field, line_axis - field.ndim)


def couplings(zone_ids, flow_speed, fixed_cells, dispersivity):
    opened = 1.0 - fixed_cells.astype(jnp.float32)
    longit = jnp.zeros(flow_speed.shape, jnp.float32)
    transv = jnp.zeros(flow_speed.shape, jnp.float32)
    for number in range(dispersivity.shape[1]):
        matched = zone_ids == number
        longit = jnp.where(matched, dispersivity[0, number], longit)
        transv = jnp.where(matched, dispersivity[1, number], transv)
    return (opened * longit * flow_speed, opened * transv * flow_speed)


def block_parts(field, coupling, line_axis):
    length = field.shape[line_axis]
    places = lax.broadcasted_iota(jnp.int32, field.shape, line_axis)
    firsts = (places == 0).astype(jnp.float32)
    lasts = (places == length - 1).astype(jnp.float32)
    stacked = jnp.stack([field, firsts, lasts])
    solved = reduce_lines(
        -coupling, 1.0 + 2.0 * coupling, -coupling, stacked, line_axis - field.ndim
    )
    interior = solved[0]
    weight_low = lax.index_in_dim(coupling, 0, line_axis, keepdims=True) * solved[1]
    weight_high = lax.index_in_dim(coupling, length - 1, line_axis, keepdims=True) * solved[2]
    edges = jnp.stack(
        [
            lax.index_in_dim(interior, 0, line_axis, keepdims=False),
            lax.index_in_dim(interior, length - 1, line_axis, keepdims=False),
            lax.index_in_dim(weight_low, 0, line_axis, keepdims=False),
            lax.index_in_dim(weight_low, length - 1, line_axis, keepdims=False),
            lax.index_in_dim(weight_high, 0, line_axis, keepdims=False),
            lax.index_in_dim(weight_high, length - 1, line_axis, keepdims=False),
        ]
    )[None]
    return (interior, weight_low, weight_high, edges)


def assemble(interior, weight_low, weight_high, gathered, position, line_axis):
    blocks = gathered.shape[0]
    zeros = jnp.zeros(gathered.shape[2:], jnp.float32)

    def forward(carry, block):
        ratio_prev, last_prev = carry
        first_low = -block[2]
        last_low = -block[3]
        first_high = -block[4]
        last_high = -block[5]
        pivot = 1.0 - first_low * ratio_prev
        factor_first = first_high / pivot
        factor_last = last_high + last_low * ratio_prev * factor_first
        value_first = (block[0] - first_low * last_prev) / pivot
        value_last = last_low * ratio_prev * value_first + block[1] - last_low * last_prev
        return ((factor_last, value_last), (factor_first, factor_last, value_first, value_last))

    _, factors = lax.scan(forward, (zeros, zeros), gathered)

    def backward(first_next, block):
        first_here = block[2] - block[0] * first_next
        last_here = block[3] - block[1] * first_next
        return (first_here, (first_here, last_here))

    _, (firsts, lasts) = lax.scan(backward, zeros, factors, reverse=True)
    last_before = lax.dynamic_index_in_dim(
        lasts, jnp.maximum(position - 1, 0), 0, keepdims=False
    ) * (position > 0).astype(jnp.float32)
    first_after = lax.dynamic_index_in_dim(
        firsts, jnp.minimum(position + 1, blocks - 1), 0, keepdims=False
    ) * (position < blocks - 1).astype(jnp.float32)
    return (
        interior
        + weight_low * jnp.expand_dims(last_before, line_axis)
        + weight_high * jnp.expand_dims(first_after, line_axis)
    )


def per_device(salinity, zone_ids, flow_speed, fixed_cells, dispersivity):
    long_coupling, trans_coupling = couplings(zone_ids, flow_speed, fixed_cells, dispersivity)
    first = line_solve(long_coupling, salinity, 2)
    field = lax.all_to_all(first, "col", split_axis=2, concat_axis=1, tiled=True)
    coupling = lax.all_to_all(trans_coupling, "col", split_axis=2, concat_axis=1, tiled=True)
    interior, weight_low, weight_high, edges = block_parts(field, coupling, 1)
    gathered = lax.all_gather(edges, "grp", axis=0, tiled=True)
    second = assemble(interior, weight_low, weight_high, gathered, lax.axis_index("grp"), 1)
    whole_field, whole_coupling = (
        lax.all_gather(second, "lay", axis=0, tiled=True),
        lax.all_gather(coupling, "lay", axis=0, tiled=True),
    )
    solved = line_solve(whole_coupling, whole_field, 0)
    start = lax.axis_index("lay") * second.shape[0]
    return lax.dynamic_slice_in_dim(solved, start, second.shape[0], 0)


def solution(mesh):
    placed = (
        P("lay", ("grp", "col"), None),
        P("lay", ("grp", "col"), None),
        P("lay", ("grp", "col"), None),
        P("lay", ("grp", "col"), None),
        P(),
    )
    return jax.shard_map(
        per_device, mesh=mesh, in_specs=placed, out_specs=P("lay", "grp", "col"), check_vma=False
    )
```

profile of v0, /device:TPU:1, one launch (start us, length us, event | category | flops | bytes accessed | tf_op | source)
XLA Modules:
  0.0 267.7 jit_solution(5317091718694986826)
XLA Ops:
  8.5 7.0 %multiply_add_fusion.8 = (f32[4,16,2048]{2,1,0:T(8,128)S(1)}, f32[4,16,2048]{2,1,0:T(8,128)S(1)}, pred[4,16,2048]{2,1,0:T(8,128)(4,1)S(1)}, pred[4,16,2048]{2,1,...) fusion(f32[4,16,2048]{2,1,0:T(8,128)} %param.17, ...), kind=kLoop, calls=%fused_computation.82 | loop fusion | flops 2883584 | bytes 3670048 | tf_op jit(solution)/shard_map/add | solution.py:46
  15.6 5.5 %multiply_multiply_fusion.1 = f32[4,16,2048]{2,1,0:T(8,128)S(1)} fusion(f32[4,16,2048]{2,1,0:T(8,128)S(1)} %copy-done.2, pred[4,16,2048]{2,1,0:T(8,128)(4,1)S(1)} %get-tuple-element.469, pred[4,16,2048]{2,1,0:T(8,128)(4,1)S(1)} %get-tuple-element.468, pred[4,16,2048]{2,1,0:T(8,128)(4,1)S(1)} %get-tuple-element.467, ...), kind=kLoop, calls=%fused_computation.85 | loop fusion | flops 1572864 | bytes 2621472 | tf_op jit(solution)/shard_map/mul | solution.py:57
  24.1 5.4 %reshape.35 = f32[16,1,8192]{2,1,0:T(1,128)} reshape(f32[2048,4,16]{2,1,0:T(4,128)} %bitcast.161) | data formatting | bytes 1048576
  29.5 7.5 %all-to-all-start = ((f32[16,1,8192]{2,1,0:T(1,128)}), f32[16,1,8192]{2,1,0:T(1,128)S(1)}, u32[]{:S(2)}, u32[]{:S(2)}) async-start(f32[16,1,8192]{2,1,0:T(1,128)} %reshape.35), calls=%async_computation | async-start | bytes 1048576 | tf_op jit(solution)/shard_map/all_to_all | solution.py:127
  37.1 22.1 %while.94 = (s32[]{:T(128)}, f32[4,16,2048]{2,1,0:T(8,128)S(1)}, f32[4,16,2048]{2,1,0:T(8,128)S(1)}, f32[4,16,2048]{2,1,0:T(8,128)S(1)}, f32[4,16,2048]{2,1,0:T(...) while((s32[]{:T(128)}, f32[4,16,2048]{2,1,0:T(8,128)S(1)}, ...), condition=%wide.region_1.2_spmd, body=%wide.region_0.1_spmd.sunk | while | flops 4980748 | bytes 18874640 | solution.py:39
  62.4 5.4 %reshape.37 = f32[16,1,8192]{2,1,0:T(1,128)} reshape(f32[2048,4,16]{2,1,0:T(4,128)} %bitcast.162) | data formatting | bytes 1048576
  67.8 5.7 %all-to-all-start.1 = ((f32[16,1,8192]{2,1,0:T(1,128)}), f32[16,1,8192]{2,1,0:T(1,128)S(1)}, u32[]{:S(2)}, u32[]{:S(2)}) async-start(f32[16,1,8192]{2,1,0:T(1,128)} %reshape.37), calls=%async_computation.1 | async-start | bytes 1048576 | tf_op jit(solution)/shard_map/all_to_all | solution.py:126
  76.2 4.2 %reshape.36 = f32[2048,4,16]{2,1,0:T(4,128)} reshape(f32[16,8192]{1,0:T(8,128)S(1)} %reduce) | data formatting | bytes 1048576
  80.4 4.4 %copy.58 = f32[4,16,16,128]{3,2,1,0:T(8,128)} copy(f32[4,16,16,128]{2,0,3,1:T(4,128)} %bitcast.163) | data formatting | bytes 1048576 | tf_op jit(solution)/shard_map/all_to_all | solution.py:127
  88.9 4.2 %reshape.38 = f32[2048,4,16]{2,1,0:T(4,128)} reshape(f32[16,8192]{1,0:T(8,128)S(1)} %reduce.1) | data formatting | bytes 1048576
  93.2 4.5 %copy.60 = f32[4,16,16,128]{3,2,1,0:T(8,128)} copy(f32[4,16,16,128]{2,0,3,1:T(4,128)} %bitcast.164) | data formatting | bytes 1048576 | tf_op jit(solution)/shard_map/all_to_all | solution.py:126
  98.8 25.8 %while.95 = (s32[]{:T(128)}, f32[4,256,128]{2,1,0:T(8,128)S(1)}, f32[4,256,128]{2,1,0:T(8,128)S(1)}, f32[4,256,128]{2,1,0:T(8,128)S(1)}, f32[3,4,256,128]{3,2,1,...) while((s32[]{:T(128)}, f32[4,256,128]{2,1,0:T(8,128)S(1)}, ...), condition=%wide.region_3.4_spmd, body=%wide.region_2.3_spmd.sunk | while | flops 7602188 | bytes 33554724 | solution.py:39
  126.3 13.8 %all-gather = f32[24,4,128]{2,1,0:T(4,128)S(1)} all-gather(f32[6,4,128]{2,1,0:T(4,128)S(1)} %constant_dynamic-update-slice_fusion.4), channel_id=2, replica_groups=mesh['grp'=4,'col'=16,'lay'=4] {'grp'}, dimensions={0}, use_global_device_ids=true | all-gather | bytes 61440 | tf_op jit(solution)/shard_map/all_gather | solution.py:129
  141.7 3.4 %multiply_add_fusion.6 = (f32[16,256,128]{2,1,0:T(8,128)}, f32[16,256,128]{2,1,0:T(8,128)S(1)}) fusion(f32[16,256,128]{2,1,0:T(8,128)} %all-gather.4.cloned.1.call-done), kind=kLoop, calls=%fused_computation.72 | loop fusion | flops 1572864 | bytes 6291456 | tf_op jit(solution)/shard_map/add | solution.py:46
  146.5 30.4 %all-gather.6.cloned.1.call-done = f32[16,256,128]{2,1,0:T(8,128)} async-done(((f32[4,256,128]{2,1,0:T(8,128)}), f32[16,256,128]{2,1,0:T(8,128)}) %all-gather.6.cloned.1.call-update) | async-done | bytes 2097168 | tf_op jit(solution)/shard_map/all_gather | solution.py:132
  176.9 81.9 %while.96 = (s32[]{:T(128)}, f32[16,256,128]{2,1,0:T(8,128)S(1)}, f32[16,256,128]{2,1,0:T(8,128)}, f32[16,256,128]{2,1,0:T(8,128)}, f32[16,256,128]{2,1,0:T(8,12...) while((s32[]{:T(128)}, f32[16,256,128]{2,1,0:T(8,128)S(1)}, ...), condition=%wide.region_9.10_spmd, body=%wide.region_8.9_spmd.sunk | while | flops 19922956 | bytes 83886376 | solution.py:39
  180.8 7.8 %pad_maximum_fusion.29 = (f32[48,256,128]{2,1,0:T(8,128)S(1)}, f32[48,256,128]{2,1,0:T(8,128)}, f32[48,256,128]{2,1,0:T(8,128)}) fusion(f32[16,256,128]{2,1,0:T(8,128)} %broadcast.149, f32[16,256,128]{2,1,0:T(8,128)} %get-tuple-element.970, f32[16,256,128]{2,1,0:T(8,128)} %get-tuple-element.969, f32[16,256,128]{2,1,0:T(8,128)S(1)} %get-tuple-element.967), kind=kLoop, calls=%fused_computation.25.clone.1 | loop fusion | flops 9437184 | bytes 27262976 | tf_op jit(solution)/shard_map/while/body/eval_jaxpr/concatenate | solution.py:13
  188.6 8.8 %dynamic-slice_multiply_fusion.13 = (f32[16,256,128]{2,1,0:T(8,128)}, f32[16,256,128]{2,1,0:T(8,128)}, f32[16,256,128]{2,1,0:T(8,128)S(1)}, f32[16,256,128]{2,1,0:T(8,128)}) fusion(f32[48,256,128]{2,1,0:T(8,128)} %get-tuple-element.758, s32[]{:T(128)S(6)} %select_n.145, f32[48,256,128]{2,1,0:T(8,128)S(1)} %pad_maximum_fusion.30, ...), kind=kLoop, calls=%fused_computation.33.clone.1 | loop fusion | flops 7340032 | bytes 33554440 | tf_op jit(solution)/shard_map/while/body/eval_jaxpr/mul | solution.py:26
  201.3 7.8 %pad_maximum_fusion.29 = (f32[48,256,128]{2,1,0:T(8,128)S(1)}, f32[48,256,128]{2,1,0:T(8,128)}, f32[48,256,128]{2,1,0:T(8,128)}) fusion(f32[16,256,128]{2,1,0:T(8,128)} %broadcast.149, f32[16,256,128]{2,1,0:T(8,128)} %get-tuple-element.970, f32[16,256,128]{2,1,0:T(8,128)} %get-tuple-element.969, f32[16,256,128]{2,1,0:T(8,128)S(1)} %get-tuple-element.967), kind=kLoop, calls=%fused_computation.25.clone.1 | loop fusion | flops 9437184 | bytes 27262976 | tf_op jit(solution)/shard_map/while/body/eval_jaxpr/concatenate | solution.py:13
  209.1 8.8 %dynamic-slice_multiply_fusion.13 = (f32[16,256,128]{2,1,0:T(8,128)}, f32[16,256,128]{2,1,0:T(8,128)}, f32[16,256,128]{2,1,0:T(8,128)S(1)}, f32[16,256,128]{2,1,0:T(8,128)}) fusion(f32[48,256,128]{2,1,0:T(8,128)} %get-tuple-element.758, s32[]{:T(128)S(6)} %select_n.145, f32[48,256,128]{2,1,0:T(8,128)S(1)} %pad_maximum_fusion.30, ...), kind=kLoop, calls=%fused_computation.33.clone.1 | loop fusion | flops 7340032 | bytes 33554440 | tf_op jit(solution)/shard_map/while/body/eval_jaxpr/mul | solution.py:26
  221.8 7.8 %pad_maximum_fusion.29 = (f32[48,256,128]{2,1,0:T(8,128)S(1)}, f32[48,256,128]{2,1,0:T(8,128)}, f32[48,256,128]{2,1,0:T(8,128)}) fusion(f32[16,256,128]{2,1,0:T(8,128)} %broadcast.149, f32[16,256,128]{2,1,0:T(8,128)} %get-tuple-element.970, f32[16,256,128]{2,1,0:T(8,128)} %get-tuple-element.969, f32[16,256,128]{2,1,0:T(8,128)S(1)} %get-tuple-element.967), kind=kLoop, calls=%fused_computation.25.clone.1 | loop fusion | flops 9437184 | bytes 27262976 | tf_op jit(solution)/shard_map/while/body/eval_jaxpr/concatenate | solution.py:13
  229.6 8.7 %dynamic-slice_multiply_fusion.13 = (f32[16,256,128]{2,1,0:T(8,128)}, f32[16,256,128]{2,1,0:T(8,128)}, f32[16,256,128]{2,1,0:T(8,128)S(1)}, f32[16,256,128]{2,1,0:T(8,128)}) fusion(f32[48,256,128]{2,1,0:T(8,128)} %get-tuple-element.758, s32[]{:T(128)S(6)} %select_n.145, f32[48,256,128]{2,1,0:T(8,128)S(1)} %pad_maximum_fusion.30, ...), kind=kLoop, calls=%fused_computation.33.clone.1 | loop fusion | flops 7340032 | bytes 33554440 | tf_op jit(solution)/shard_map/while/body/eval_jaxpr/mul | solution.py:26
  242.1 7.8 %pad_maximum_fusion.29 = (f32[48,256,128]{2,1,0:T(8,128)S(1)}, f32[48,256,128]{2,1,0:T(8,128)}, f32[48,256,128]{2,1,0:T(8,128)}) fusion(f32[16,256,128]{2,1,0:T(8,128)} %broadcast.149, f32[16,256,128]{2,1,0:T(8,128)} %get-tuple-element.970, f32[16,256,128]{2,1,0:T(8,128)} %get-tuple-element.969, f32[16,256,128]{2,1,0:T(8,128)S(1)} %get-tuple-element.967), kind=kLoop, calls=%fused_computation.25.clone.1 | loop fusion | flops 9437184 | bytes 27262976 | tf_op jit(solution)/shard_map/while/body/eval_jaxpr/concatenate | solution.py:13
  249.9 8.8 %dynamic-slice_multiply_fusion.13 = (f32[16,256,128]{2,1,0:T(8,128)}, f32[16,256,128]{2,1,0:T(8,128)}, f32[16,256,128]{2,1,0:T(8,128)S(1)}, f32[16,256,128]{2,1,0:T(8,128)}) fusion(f32[48,256,128]{2,1,0:T(8,128)} %get-tuple-element.758, s32[]{:T(128)S(6)} %select_n.145, f32[48,256,128]{2,1,0:T(8,128)S(1)} %pad_maximum_fusion.30, ...), kind=kLoop, calls=%fused_computation.33.clone.1 | loop fusion | flops 7340032 | bytes 33554440 | tf_op jit(solution)/shard_map/while/body/eval_jaxpr/mul | solution.py:26
  (202 shorter events, 84.8 us)
Async XLA Ops:
  6.5 9.0 %copy-start.2 = (f32[4,16,2048]{2,1,0:T(8,128)S(1)}, f32[4,16,2048]{2,1,0:T(8,128)}, u32[]{:S(2)}) copy-start(f32[4,16,2048]{2,1,0:T(8,128)} %param.17) | copy-start | bytes 1572868
  6.5 9.0 %copy-start.3 = (s32[4,16,2048]{2,1,0:T(8,128)S(1)}, s32[4,16,2048]{2,1,0:T(8,128)}, u32[]{:S(2)}) copy-start(s32[4,16,2048]{2,1,0:T(8,128)} %param.18) | copy-start | bytes 1572868
  29.5 7.6 %copy-start.1 = (f32[4,16,2048]{2,1,0:T(8,128)S(1)}, f32[4,16,2048]{2,1,0:T(8,128)}, u32[]{:S(2)}) copy-start(f32[4,16,2048]{2,1,0:T(8,128)} %param.15) | copy-start | bytes 1572868
  29.5 38.3 %all-to-all-start = ((f32[16,1,8192]{2,1,0:T(1,128)}), f32[16,1,8192]{2,1,0:T(1,128)S(1)}, u32[]{:S(2)}, u32[]{:S(2)}) async-start(f32[16,1,8192]{2,1,0:T(1,128)} %reshape.35), calls=%async_computation | async-start | bytes 1048576 | tf_op jit(solution)/shard_map/all_to_all | solution.py:127
  67.8 19.2 %all-to-all-start.1 = ((f32[16,1,8192]{2,1,0:T(1,128)}), f32[16,1,8192]{2,1,0:T(1,128)S(1)}, u32[]{:S(2)}, u32[]{:S(2)}) async-start(f32[16,1,8192]{2,1,0:T(1,128)} %reshape.37), calls=%async_computation.1 | async-start | bytes 1048576 | tf_op jit(solution)/shard_map/all_to_all | solution.py:126
  73.6 68.2 %all-gather.4.cloned.1.call-start = ((), (), s32[]{:S(2)}) async-start(), calls=%async_computation.2 | async-start | bytes 2621440 | tf_op jit(solution)/shard_map/all_gather | solution.py:133
  84.9 92.0 %all-gather.6.cloned.1.call-start = ((), (), s32[]{:S(2)}) async-start(), calls=%async_computation.3 | async-start | bytes 2621440 | tf_op jit(solution)/shard_map/all_gather | solution.py:132
  97.6 1.1 copy-start.4
  176.9 1.6 copy-start
  197.4 1.6 copy-start
  217.9 1.6 copy-start
  238.3 1.6 copy-start
Sparse Core Ops, SparseCore 0:
  85.0 35.0 all-gather.3
  141.8 35.0 all-gather.5
where the time goes:
time: 269 us; the launch traced here: 268 us
  other arithmetic  138 us (51%)
  local copies, waits for them, and re-layouts  56.2 us (21%)
  waiting for transfers between devices  30.5 us (11%)
  blocking collectives  13.8 us (5%)
  between operations  13.7 us (5%)
  starting transfers between devices  13.5 us (5%)
    mul x23, other arithmetic, one_level(): above_next = weight_above * shifted(above_now, stride, line_axis, 0.0, 1)  51.2 us
    concatenate x35, other arithmetic, shifted(): padded = jnp.concatenate([padding, values, padding], axis=line_axis)  47.4 us
    all_gather x1, waiting for transfers between devices, per_device(): lax.all_gather(second, 'lay', axis=0, tiled=True)  30.4 us
    unnamed x20, local copies, waits for them, and re-layouts  21.7 us
    all_gather x1, blocking collectives, per_device(): gathered = lax.all_gather(edges, 'grp', axis=0, tiled=True)  13.8 us
    add x8, other arithmetic, one_level(): right_now + weight_below * shifted(right_now, stride, line_axis, 0.0, -1)  10.8 us
    add x2, other arithmetic, line_solve(): 1.0 + 2.0 * coupling  10.4 us
    another operation x60, local copies, waits for them, and re-layouts  9.29 us
  transfers between devices with their start and end apart: 4, of which 1 were waited for; matrix products, arithmetic and copies ran while one was open for 32% of the time, Pallas kernels for 0%

commit v1 on v0

v1 whole, which is shorter than its diff:
```python
import jax
import jax.numpy as jnp
from jax import lax
from jax.experimental import pallas as pl
from jax.experimental.pallas import tpu as pltpu
from jax.sharding import PartitionSpec as P

NCOL = 16
NGRP = 4
NLAY = 4
L = 4
RB = 16
LINES = L * RB
LANES = 128
STEP = 16
ROWS = NCOL * RB
ZCH = 4
ZR = ROWS // ZCH
FCH = 2
FL = L // FCH
MESH = pl.DeviceIdType.MESH
F32 = jnp.float32


def butterfly(parts, lane):
    parts = list(parts)
    for m in range(4):
        step = 1 << m
        high = (lane & step) != 0
        for i in range(16):
            if i & step:
                continue
            a, b = parts[i], parts[i + step]
            parts[i] = jnp.where(high, pltpu.roll(b, step, 1), a)
            parts[i + step] = jnp.where(high, b, pltpu.roll(a, LANES - step, 1))
    return parts


def pick(zone, table):
    for m in range(3):
        bit = (zone & (1 << m)) != 0
        table = [jnp.where(bit, table[i + 1], table[i]) for i in range(0, len(table), 2)]
    return table[0]


def kernel(
    sal_hbm, zone_hbm, flow_hbm, fixed_hbm, disp_ref, out_hbm,
    sal, zone, flow, fixed,
    long_nat, st, ft, ys, yf,
    us, uf, up, uq, ur,
    yd, yfd, yp, yw, yr, lev_a, lev_c, lev_i, tmp,
    gcoef, gval,
    sec, wu, pu, wd, pd, eu_in, ed_in, eu_out, ed_out, qu_in, qd_in, qu_out, qd_out, res,
    in_sem, s_send, s_recv, f_send, f_recv, gc_send, gc_recv, gv_send, gv_recv,
    e_send, e_recv, q_send, q_recv, out_sem,
):
    grp = lax.axis_index("grp")
    col = lax.axis_index("col")
    lay = lax.axis_index("lay")

    loads = [
        pltpu.make_async_copy(zone_hbm, zone, in_sem.at[0]),
        pltpu.make_async_copy(flow_hbm, flow, in_sem.at[1]),
        pltpu.make_async_copy(fixed_hbm, fixed, in_sem.at[2]),
        pltpu.make_async_copy(sal_hbm, sal, in_sem.at[3]),
    ]
    for copy in loads:
        copy.start()

    barrier = pltpu.get_barrier_semaphore()

    def greet_col(o, carry):
        pl.semaphore_signal(barrier, inc=1, device_id={"col": (col + o) % NCOL}, device_id_type=MESH)
        return carry

    lax.fori_loop(1, NCOL, greet_col, 0)
    for o in range(1, NGRP):
        pl.semaphore_signal(barrier, inc=1, device_id={"grp": (grp + o) % NGRP}, device_id_type=MESH)
    for o in (1, NLAY - 1):
        pl.semaphore_signal(barrier, inc=1, device_id={"lay": (lay + o) % NLAY}, device_id_type=MESH)

    lane = lax.broadcasted_iota(jnp.int32, (8, LANES), 1)

    for copy in loads[:3]:
        copy.wait()
    table_long = [disp_ref[0, i] for i in range(8)]
    table_trans = [disp_ref[1, i] for i in range(8)]

    def couple(z, carry):
        for half in range(2):
            rows = pl.ds(8 * half, 8)
            for b in range(NCOL):
                cols = pl.ds(LANES * b, LANES)
                ids = zone[z, rows, cols]
                speed = flow[z, rows, cols]
                opened = 1.0 - fixed[z, rows, cols].astype(F32)
                st[b, z, rows, :] = opened * pick(ids, table_trans) * speed
                long_nat[b, z, rows, :] = opened * pick(ids, table_long) * speed
        return carry

    lax.fori_loop(0, L, couple, 0)

    pl.semaphore_wait(barrier, NCOL - 1 + NGRP - 1 + 2)

    def s_copy(dest, source):
        return pltpu.make_async_remote_copy(
            src_ref=st.at[dest],
            dst_ref=ys.at[:, pl.ds(source * RB, RB), :],
            send_sem=s_send.at[dest],
            recv_sem=s_recv.at[source],
            device_id={"col": dest},
            device_id_type=MESH,
        )

    def s_start(o, carry):
        s_copy((col + o) % NCOL, col).start()
        return carry

    lax.fori_loop(1, NCOL, s_start, 0)
    ys[:, pl.ds(col * RB, RB), :] = st[col]

    loads[3].wait()

    def spread(z, carry):
        for half in range(2):
            rows = pl.ds(8 * half, 8)
            line = pl.ds(pl.multiple_of(z * RB + 8 * half, 8), 8)
            s_parts = butterfly([long_nat[b, z, rows, :] for b in range(NCOL)], lane)
            for j in range(STEP):
                us[j, line, :] = s_parts[j]
            f_parts = butterfly([sal[z, rows, pl.ds(LANES * b, LANES)] for b in range(NCOL)], lane)
            for j in range(STEP):
                uf[j, line, :] = f_parts[j]
        return carry

    lax.fori_loop(0, L, spread, 0)

    whole = (LINES, LANES)
    e = jnp.ones(whole, F32)
    r = jnp.ones(whole, F32)
    q = jnp.zeros(whole, F32)
    alpha = jnp.zeros(whole, F32)
    eb = jnp.ones(whole, F32)
    for j in range(1, STEP):
        s = us[j]
        f = uf[j]
        se = s * e
        w = 1.0 / (1.0 + s + se)
        p = s * w
        e = (1.0 + se) * w
        q = f * w + p * q
        r_now = r * p
        alpha = alpha + r * q
        eb = eb - r * r_now
        r = r_now
        up[j] = p
        uq[j] = q
        ur[j] = r

    lanes = lax.broadcasted_iota(jnp.int32, whole, 1)
    sub = lanes // 16
    low = lanes % 16
    first_block = lanes == 0
    last_block = lanes == LANES - 1

    def before(v, d):
        if d >= 8:
            return pltpu.roll(v, d // 8, 1)
        return jnp.where(sub >= d, pltpu.roll(v, 16 * d, 1), pltpu.roll(v, 16 * d + 1, 1))

    def after(v, d):
        if d >= 8:
            return pltpu.roll(v, LANES - d // 8, 1)
        return jnp.where(
            sub < 8 - d, pltpu.roll(v, LANES - 16 * d, 1), pltpu.roll(v, LANES - 16 * d - 1, 1)
        )

    s = us[0]
    ep_left = jnp.where(first_block, 1.0, before(e, 1))
    q_left = jnp.where(first_block, 0.0, before(q, 1))
    r_left = jnp.where(first_block, 0.0, before(r, 1))
    inv = 1.0 / (1.0 + s * (eb + ep_left))
    a = s * r_left * inv
    c = jnp.where(last_block, 0.0, s * r * inv)
    f = (uf[0] + s * (q_left + alpha)) * inv
    for m in range(7):
        d = 1 << m
        inv = 1.0 / (1.0 - a * before(c, d) - c * after(a, d))
        f = (f + a * before(f, d) + c * after(f, d)) * inv
        if m < 6:
            a, c = a * before(a, d) * inv, c * after(c, d) * inv
    uf[0] = f
    x = jnp.where(last_block, 0.0, after(f, 1))
    for j in range(STEP - 1, 0, -1):
        x = uq[j] + ur[j] * f + up[j] * x
        uf[j] = x

    def f_copy(chunk, dest, source):
        return pltpu.make_async_remote_copy(
            src_ref=ft.at[dest, pl.ds(chunk * FL, FL)],
            dst_ref=yf.at[pl.ds(chunk * FL, FL), pl.ds(source * RB, RB), :],
            send_sem=f_send.at[chunk, dest],
            recv_sem=f_recv.at[chunk, source],
            device_id={"col": dest},
            device_id_type=MESH,
        )

    for chunk in range(FCH):

        def gather(z, carry):
            for half in range(2):
                rows = pl.ds(8 * half, 8)
                line = pl.ds(pl.multiple_of(z * RB + 8 * half, 8), 8)
                parts = butterfly([uf[j, line, :] for j in range(STEP)], lane)
                for b in range(NCOL):
                    ft[b, z, rows, :] = parts[b]
            return carry

        lax.fori_loop(chunk * FL, (chunk + 1) * FL, gather, 0)

        def f_start(o, carry):
            f_copy(chunk, (col + o) % NCOL, col).start()
            return carry

        lax.fori_loop(1, NCOL, f_start, 0)
        layers = pl.ds(chunk * FL, FL)
        yf[layers, pl.ds(col * RB, RB), :] = ft[col, layers]

    def s_wait(o, carry):
        s_copy(col, (col + NCOL - o) % NCOL).wait_recv()
        return carry

    lax.fori_loop(1, NCOL, s_wait, 0)

    def rows_of(z, h, j):
        return (z, pl.ds(128 * h + j, 8, stride=STEP), slice(None))

    for z in range(L):
        for h in range(2):
            for j in range(STEP):
                yd[j, pl.ds(16 * z + 8 * h, 8), :] = ys[rows_of(z, h, j)]

    e = jnp.ones(whole, F32)
    r = jnp.ones(whole, F32)
    eb = jnp.ones(whole, F32)
    for j in range(1, STEP):
        s = yd[j]
        se = s * e
        w = 1.0 / (1.0 + s + se)
        p = s * w
        e = (1.0 + se) * w
        r_now = r * p
        eb = eb - r * r_now
        r = r_now
        yw[j] = w
        yp[j] = p
        yr[j] = r
    block = lax.broadcasted_iota(jnp.int32, whole, 0) % RB

    def above(v, d, edge):
        return jnp.where(block >= d, pltpu.roll(v, d, 0), edge)

    def below(v, d, edge):
        return jnp.where(block < RB - d, pltpu.roll(v, LINES - d, 0), edge)

    s = yd[0]
    inv = 1.0 / (1.0 + s * (eb + above(e, 1, 1.0)))
    a = s * above(r, 1, 1.0) * inv
    c = s * r * inv
    yw[0] = inv
    for m in range(4):
        d = 1 << m
        inv = 1.0 / (1.0 - a * above(c, d, 0.0) - c * below(a, d, 0.0))
        lev_a[m] = a * inv
        lev_c[m] = c * inv
        lev_i[m] = inv
        a, c = a * above(a, d, 1.0) * inv, c * below(c, d, 1.0) * inv
    lev_a[4] = a
    lev_c[4] = c
    top = pl.ds(0, L, stride=RB)
    bottom = pl.ds(RB - 1, L, stride=RB)
    tmp[0] = r * a
    tmp[1] = (1.0 - e) + r * c
    gcoef[grp, 0] = lev_a[4, top, :]
    gcoef[grp, 1] = lev_c[4, top, :]
    gcoef[grp, 2] = tmp[0, bottom, :]
    gcoef[grp, 3] = tmp[1, bottom, :]

    def g_copy(buf, send, recv, dest, source):
        return pltpu.make_async_remote_copy(
            src_ref=buf.at[source],
            dst_ref=buf.at[source],
            send_sem=send.at[dest],
            recv_sem=recv.at[source],
            device_id={"grp": dest},
            device_id_type=MESH,
        )

    for o in range(1, NGRP):
        g_copy(gcoef, gc_send, gc_recv, (grp + o) % NGRP, grp).start()

    def e_copy(way, c, dest):
        rows = pl.ds(pl.multiple_of(c * ZR, ZR), ZR)
        src, dst = ((eu_out, eu_in), (ed_out, ed_in))[way]
        return pltpu.make_async_remote_copy(
            src_ref=src.at[rows],
            dst_ref=dst.at[rows],
            send_sem=e_send.at[way, c],
            recv_sem=e_recv.at[way, c],
            device_id={"lay": dest},
            device_id_type=MESH,
        )

    def q_copy(way, c, dest):
        rows = pl.ds(pl.multiple_of(c * ZR, ZR), ZR)
        src, dst = ((qu_out, qu_in), (qd_out, qd_in))[way]
        return pltpu.make_async_remote_copy(
            src_ref=src.at[rows],
            dst_ref=dst.at[rows],
            send_sem=q_send.at[way, c],
            recv_sem=q_recv.at[way, c],
            device_id={"lay": dest},
            device_id_type=MESH,
        )

    @pl.when(lay == 0)
    def _():
        eu_in[...] = jnp.ones((ROWS, LANES), F32)
        qu_in[...] = jnp.zeros((ROWS, LANES), F32)

    @pl.when(lay == NLAY - 1)
    def _():
        ed_in[...] = jnp.ones((ROWS, LANES), F32)
        qd_in[...] = jnp.zeros((ROWS, LANES), F32)

    def e_step(t, carry):
        for way in range(2):
            back = lay if way == 0 else NLAY - 1 - lay
            dest = jnp.minimum(lay + 1, NLAY - 1) if way == 0 else jnp.maximum(lay - 1, 0)
            c = t - back

            @pl.when((c >= 0) & (c < ZCH))
            def _():
                rows = pl.ds(pl.multiple_of(c * ZR, ZR), ZR)
                src, out, wr, pr = ((eu_in, eu_out, wu, pu), (ed_in, ed_out, wd, pd))[way]

                @pl.when(back > 0)
                def _():
                    e_copy(way, c, dest).wait_recv()

                e = src[rows, :]
                for i in range(L) if way == 0 else range(L - 1, -1, -1):
                    s = ys[i, rows, :]
                    se = s * e
                    w = 1.0 / (1.0 + s + se)
                    e = (1.0 + se) * w
                    wr[i, rows, :] = w
                    pr[i, rows, :] = s * w
                out[rows, :] = e

                @pl.when(back < NLAY - 1)
                def _():
                    e_copy(way, c, dest).start()

        return carry

    lax.fori_loop(0, ZCH + NLAY - 1, e_step, 0)

    for chunk in range(FCH):

        def f_wait(o, carry):
            f_copy(chunk, col, (col + NCOL - o) % NCOL).wait_recv()
            return carry

        lax.fori_loop(1, NCOL, f_wait, 0)
        for z in range(chunk * FL, (chunk + 1) * FL):
            for h in range(2):
                for j in range(STEP):
                    yfd[j, pl.ds(16 * z + 8 * h, 8), :] = yf[rows_of(z, h, j)]

    q = yfd[1] * yw[1]
    yfd[1] = q
    alpha = q
    for j in range(2, STEP):
        q = yfd[j] * yw[j] + yp[j] * q
        yfd[j] = q
        alpha = alpha + yr[j - 1] * q
    f = (yfd[0] + yd[0] * (above(q, 1, 0.0) + alpha)) * yw[0]
    for m in range(4):
        d = 1 << m
        f = f * lev_i[m] + lev_a[m] * above(f, d, 0.0) + lev_c[m] * below(f, d, 0.0)
    tmp[2] = f
    tmp[3] = q + yr[STEP - 1] * f
    gval[grp, 0] = tmp[2, top, :]
    gval[grp, 1] = tmp[3, bottom, :]
    for o in range(1, NGRP):
        g_copy(gval, gv_send, gv_recv, (grp + o) % NGRP, grp).start()
    for o in range(1, NGRP):
        g_copy(gcoef, gc_send, gc_recv, grp, (grp + NGRP - o) % NGRP).wait_recv()
    for o in range(1, NGRP):
        g_copy(gval, gv_send, gv_recv, grp, (grp + NGRP - o) % NGRP).wait_recv()

    be = [gcoef[g, 0] for g in range(NGRP)]
    ga = [gcoef[g, 1] for g in range(NGRP)]
    rr = [gcoef[g, 2] for g in range(NGRP)]
    pp = [gcoef[g, 3] for g in range(NGRP)]
    al = [gval[g, 0] for g in range(NGRP)]
    qq = [gval[g, 1] for g in range(NGRP)]
    pre_p, pre_q = [pp[0]], [qq[0]]
    for g in range(1, NGRP - 1):
        t = rr[g] / (1.0 - pre_p[-1] * be[g])
        pre_p, pre_q = (
            pre_p + [pp[g] + t * pre_p[-1] * ga[g]],
            pre_q + [qq[g] + t * (pre_q[-1] + pre_p[-1] * al[g])],
        )
    suf_p, suf_q = [be[NGRP - 1]], [al[NGRP - 1]]
    for g in range(NGRP - 2, 0, -1):
        t = ga[g] * suf_p[0] / (1.0 - pp[g] * suf_p[0])
        suf_p, suf_q = (
            [be[g] + t * rr[g]] + suf_p,
            [al[g] + ga[g] * suf_q[0] + t * (qq[g] + pp[g] * suf_q[0])] + suf_q,
        )
    left = jnp.zeros((L, LANES), F32)
    right = jnp.zeros((L, LANES), F32)
    for i in range(NGRP - 1):
        u = (pre_q[i] + pre_p[i] * suf_q[i]) / (1.0 - pre_p[i] * suf_p[i])
        v = suf_q[i] + suf_p[i] * u
        left = jnp.where(grp == i + 1, u, left)
        right = jnp.where(grp == i, v, right)

    def per_line(v):
        return jnp.concatenate([jnp.broadcast_to(v[z : z + 1], (RB, LANES)) for z in range(L)], 0)

    right = per_line(right)
    f = f + lev_a[4] * per_line(left) + lev_c[4] * right
    x = jnp.where(block == RB - 1, right, pltpu.roll(f, LINES - 1, 0))
    for j in range(STEP - 1, -1, -1):
        if j == 0:
            x = f
        else:
            x = yfd[j] + yr[j] * f + yp[j] * x
        for z in range(L):
            for h in range(2):
                m = 16 * z + 8 * h
                sec[rows_of(z, h, j)] = x[m : m + 8]

    def q_step(t, carry):
        for way in range(2):
            back = lay if way == 0 else NLAY - 1 - lay
            dest = jnp.minimum(lay + 1, NLAY - 1) if way == 0 else jnp.maximum(lay - 1, 0)
            c = t - back

            @pl.when((c >= 0) & (c < ZCH))
            def _():
                rows = pl.ds(pl.multiple_of(c * ZR, ZR), ZR)
                src, out, wr, pr = ((qu_in, qu_out, wu, pu), (qd_in, qd_out, wd, pd))[way]
                order = range(L) if way == 0 else range(L - 1, -1, -1)

                @pl.when(back > 0)
                def _():
                    q_copy(way, c, dest).wait_recv()

                q = src[rows, :]
                for i in order:
                    q = sec[i, rows, :] * wr[i, rows, :] + pr[i, rows, :] * q
                    if way == 0:
                        res[i, rows, :] = q
                out[rows, :] = q

                @pl.when(back < NLAY - 1)
                def _():
                    q_copy(way, c, dest).start()

        c = t - jnp.maximum(lay, NLAY - 1 - lay)

        @pl.when((c >= 0) & (c < ZCH))
        def _():
            rows = pl.ds(pl.multiple_of(c * ZR, ZR), ZR)
            ep = eu_out[rows, :]
            p = 1.0 - ep
            x = (res[L - 1, rows, :] + p * qd_in[rows, :]) / (ep + p * ed_in[rows, :])
            res[L - 1, rows, :] = x
            for i in range(L - 2, -1, -1):
                x = res[i, rows, :] + pu[i, rows, :] * x
                res[i, rows, :] = x
            pltpu.make_async_copy(res.at[:, rows, :], out_hbm.at[:, rows, :], out_sem.at[c]).start()

        return carry

    lax.fori_loop(0, ZCH + NLAY - 1, q_step, 0)

    def s_done(o, carry):
        s_copy((col + o) % NCOL, col).wait_send()
        for chunk in range(FCH):
            f_copy(chunk, (col + o) % NCOL, col).wait_send()
        return carry

    lax.fori_loop(1, NCOL, s_done, 0)
    for o in range(1, NGRP):
        g_copy(gcoef, gc_send, gc_recv, (grp + o) % NGRP, grp).wait_send()
        g_copy(gval, gv_send, gv_recv, (grp + o) % NGRP, grp).wait_send()
    for c in range(ZCH):

        @pl.when(lay < NLAY - 1)
        def _():
            e_copy(0, c, jnp.minimum(lay + 1, NLAY - 1)).wait_send()
            q_copy(0, c, jnp.minimum(lay + 1, NLAY - 1)).wait_send()

        @pl.when(lay > 0)
        def _():
            e_copy(1, c, jnp.maximum(lay - 1, 0)).wait_send()
            q_copy(1, c, jnp.maximum(lay - 1, 0)).wait_send()

        rows = pl.ds(c * ZR, ZR)
        pltpu.make_async_copy(res.at[:, rows, :], out_hbm.at[:, rows, :], out_sem.at[c]).wait()


def per_device(salinity, zone_ids, flow_speed, fixed_cells, dispersivity):
    hbm = pl.BlockSpec(memory_space=pl.ANY)
    nat = (L, RB, NCOL * LANES)
    slab = (L, ROWS, LANES)
    by_dest = (NCOL, L, RB, LANES)
    steps = (STEP, LINES, LANES)
    plane = (ROWS, LANES)

    def vm(shape, dtype=F32):
        return pltpu.VMEM(shape, dtype)

    dma = pltpu.SemaphoreType.DMA
    return pl.pallas_call(
        kernel,
        out_shape=jax.ShapeDtypeStruct(slab, F32),
        in_specs=[hbm, hbm, hbm, hbm, pl.BlockSpec(memory_space=pltpu.SMEM)],
        out_specs=hbm,
        scratch_shapes=[
            vm(nat), vm(nat, jnp.int32), vm(nat), vm(nat, jnp.int32),
            vm(by_dest), vm(by_dest), vm(by_dest), vm(slab), vm(slab),
            vm(steps), vm(steps), vm(steps), vm(steps), vm(steps),
            vm(steps), vm(steps), vm(steps), vm(steps), vm(steps),
            vm((5, LINES, LANES)), vm((5, LINES, LANES)), vm((4, LINES, LANES)), vm((4, LINES, LANES)),
            vm((NGRP, 4, L, LANES)), vm((NGRP, 2, L, LANES)),
            vm(slab), vm(slab), vm(slab), vm(slab), vm(slab),
            vm(plane), vm(plane), vm(plane), vm(plane), vm(plane), vm(plane), vm(plane), vm(plane),
            vm(slab),
            dma((4,)), dma((NCOL,)), dma((NCOL,)), dma((FCH, NCOL)), dma((FCH, NCOL)),
            dma((NGRP,)), dma((NGRP,)), dma((NGRP,)), dma((NGRP,)),
            dma((2, ZCH)), dma((2, ZCH)), dma((2, ZCH)), dma((2, ZCH)), dma((ZCH,)),
        ],
        compiler_params=pltpu.CompilerParams(
            collective_id=0, has_side_effects=True, vmem_limit_bytes=56 * 1024 * 1024
        ),
        name="lod_step",
    )(salinity, zone_ids, flow_speed, fixed_cells, dispersivity)


def solution(mesh):
    placed = P("lay", ("grp", "col"), None)
    return jax.shard_map(
        per_device,
        mesh=mesh,
        in_specs=(placed, placed, placed, placed, P()),
        out_specs=P("lay", "grp", "col"),
        check_vma=False,
    )
```

time: 269 us -> 62.7 us (0.23)
  the two profiles are of different devices: /device:TPU:1 before, /device:TPU:32 now
where the time goes in v1:
time: 62.7 us; the launch traced here: 62.5 us
  Pallas kernels  60.7 us (97%)
  local copies, waits for them, and re-layouts  1.87 us (3%)
    pallas_call x1, Pallas kernels, per_device(): pl.pallas_call(kernel, out_shape=jax.ShapeDtypeStruct(slab, F32), in_spec...  60.7 us
    unnamed x1, local copies, waits for them, and re-layouts  1.87 us

profile of v1, /device:TPU:32, one launch (start us, length us, event | category | flops | bytes accessed | tf_op | source)
XLA Modules:
  0.0 62.5 jit_solution(12858354636275934630)
XLA Ops:
  0.0 60.7 %lod_step.1 = f32[4,256,128]{2,1,0:T(8,128)} custom-call(f32[4,16,2048]{2,1,0:T(8,128)} %sal_hbm.1, s32[4,16,2048]{2,1,0:T(8,128)} %zone_hbm.1, f32[4,16,2048]{2,1,0:T(8,128)} %flow_hbm.1, s32[4,16,2048]{2,1,0:T(8,128)} %fixed_hbm.1, f32[2,8]{1,0:T(2,128)} %disp_ref.1), custom_call_target="tpu_custom_call" | custom-call | tf_op jit(solution)/shard_map/lod_step/pallas_call | solution.py:530
  60.7 1.9 %copy.7 = f32[4,256,128]{2,1,0:T(8,128)} copy(f32[4,256,128]{2,1,0:T(8,128)} %lod_step.1) | data formatting | bytes 1048576

commit v2 on v1

--- a/solution.py
+++ b/solution.py
@@ -16,6 +16,8 @@
 ROWS = NCOL * RB
 ZCH = 4
 ZR = ROWS // ZCH
+QCH = 2
+QR = ROWS // QCH
 FCH = 2
 FL = L // FCH
 MESH = pl.DeviceIdType.MESH
@@ -50,13 +52,119 @@
     us, uf, up, uq, ur,
     yd, yfd, yp, yw, yr, lev_a, lev_c, lev_i, tmp,
     gcoef, gval,
-    sec, wu, pu, wd, pd, eu_in, ed_in, eu_out, ed_out, qu_in, qd_in, qu_out, qd_out, res,
+    sec, wu, pu, wd, pd, eu_in, ed_in, eu_out, ed_out, ru, rd, r_in, qu_out, qd_out, q_in, res,
     in_sem, s_send, s_recv, f_send, f_recv, gc_send, gc_recv, gv_send, gv_recv,
-    e_send, e_recv, q_send, q_recv, out_sem,
+    e_send, e_recv, r_send, r_recv, q_send, q_recv, out_sem,
 ):
     grp = lax.axis_index("grp")
     col = lax.axis_index("col")
     lay = lax.axis_index("lay")
+
+    def s_copy(dest, source):
+        return pltpu.make_async_remote_copy(
+            src_ref=st.at[dest],
+            dst_ref=ys.at[:, pl.ds(source * RB, RB), :],
+            send_sem=s_send.at[dest],
+            recv_sem=s_recv.at[source],
+            device_id={"col": dest},
+            device_id_type=MESH,
+        )
+
+    def f_copy(chunk, dest, source):
+        return pltpu.make_async_remote_copy(
+            src_ref=ft.at[dest, pl.ds(chunk * FL, FL)],
+            dst_ref=yf.at[pl.ds(chunk * FL, FL), pl.ds(source * RB, RB), :],
+            send_sem=f_send.at[chunk, dest],
+            recv_sem=f_recv.at[chunk, source],
+            device_id={"col": dest},
+            device_id_type=MESH,
+        )
+
+    def g_copy(buf, send, recv, dest, source):
+        return pltpu.make_async_remote_copy(
+            src_ref=buf.at[source],
+            dst_ref=buf.at[source],
+            send_sem=send.at[dest],
+            recv_sem=recv.at[source],
+            device_id={"grp": dest},
+            device_id_type=MESH,
+        )
+
+    def e_copy(way, c, dest):
+        rows = pl.ds(pl.multiple_of(c * ZR, ZR), ZR)
+        src, dst = ((eu_out, eu_in), (ed_out, ed_in))[way]
+        return pltpu.make_async_remote_copy(
+            src_ref=src.at[rows],
+            dst_ref=dst.at[rows],
+            send_sem=e_send.at[way, c],
+            recv_sem=e_recv.at[way, c],
+            device_id={"lay": dest},
+            device_id_type=MESH,
+        )
+
+    def r_copy(way, dest, source):
+        return pltpu.make_async_remote_copy(
+            src_ref=(ru, rd)[way],
+            dst_ref=r_in.at[source],
+            send_sem=r_send.at[dest],
+            recv_sem=r_recv.at[source],
+            device_id={"lay": dest},
+            device_id_type=MESH,
+        )
+
+    def q_copy(way, c, dest, source):
+        rows = pl.ds(pl.multiple_of(c * QR, QR), QR)
+        return pltpu.make_async_remote_copy(
+            src_ref=(qu_out, qd_out)[way].at[rows],
+            dst_ref=q_in.at[source, rows],
+            send_sem=q_send.at[c, dest],
+            recv_sem=q_recv.at[c, source],
+            device_id={"lay": dest},
+            device_id_type=MESH,
+        )
+
+    def out_copy(c):
+        rows = pl.ds(pl.multiple_of(c * QR, QR), QR)
+        return pltpu.make_async_copy(res.at[:, rows, :], out_hbm.at[:, rows, :], out_sem.at[c])
+
+    def ahead(way, k):
+        return range(k + 1, NLAY) if way == 0 else range(k - 1, -1, -1)
+
+    def e_stage(k):
+        for way in range(2):
+
+            @pl.when(lay == (k if way == 0 else NLAY - 1 - k))
+            def _():
+                me = k if way == 0 else NLAY - 1 - k
+                src, out, wr, pr, prod = ((eu_in, eu_out, wu, pu, ru), (ed_in, ed_out, wd, pd, rd))[way]
+
+                def step(c, carry):
+                    rows = pl.ds(pl.multiple_of(c * ZR, ZR), ZR)
+                    if k > 0:
+                        e_copy(way, c, me).wait_recv()
+                        e = src[rows, :]
+                    else:
+                        e = jnp.ones((ZR, LANES), F32)
+                    total = None
+                    for i in range(L) if way == 0 else range(L - 1, -1, -1):
+                        s = ys[i, rows, :]
+                        se = s * e
+                        w = 1.0 / (1.0 + s + se)
+                        e = (1.0 + se) * w
+                        p = s * w
+                        wr[i, rows, :] = w
+                        pr[i, rows, :] = p
+                        total = p if total is None else total * p
+                    out[rows, :] = e
+                    prod[rows, :] = total
+                    if k < NLAY - 1:
+                        e_copy(way, c, ahead(way, me)[0]).start()
+                    return carry
+
+                lax.fori_loop(0, ZCH, step, 0)
+                if 0 < k < NLAY - 1:
+                    for dest in ahead(way, me):
+                        r_copy(way, dest, me).start()
 
     loads = [
         pltpu.make_async_copy(zone_hbm, zone, in_sem.at[0]),
@@ -101,16 +209,6 @@
     lax.fori_loop(0, L, couple, 0)
 
     pl.semaphore_wait(barrier, NCOL - 1 + NGRP - 1 + 2)
-
-    def s_copy(dest, source):
-        return pltpu.make_async_remote_copy(
-            src_ref=st.at[dest],
-            dst_ref=ys.at[:, pl.ds(source * RB, RB), :],
-            send_sem=s_send.at[dest],
-            recv_sem=s_recv.at[source],
-            device_id={"col": dest},
-            device_id_type=MESH,
-        )
 
     def s_start(o, carry):
         s_copy((col + o) % NCOL, col).start()
@@ -189,21 +287,12 @@
         f = (f + a * before(f, d) + c * after(f, d)) * inv
         if m < 6:
             a, c = a * before(a, d) * inv, c * after(c, d) * inv
+
     uf[0] = f
     x = jnp.where(last_block, 0.0, after(f, 1))
     for j in range(STEP - 1, 0, -1):
         x = uq[j] + ur[j] * f + up[j] * x
         uf[j] = x
-
-    def f_copy(chunk, dest, source):
-        return pltpu.make_async_remote_copy(
-            src_ref=ft.at[dest, pl.ds(chunk * FL, FL)],
-            dst_ref=yf.at[pl.ds(chunk * FL, FL), pl.ds(source * RB, RB), :],
-            send_sem=f_send.at[chunk, dest],
-            recv_sem=f_recv.at[chunk, source],
-            device_id={"col": dest},
-            device_id_type=MESH,
-        )
 
     for chunk in range(FCH):
 
@@ -231,6 +320,8 @@
         return carry
 
     lax.fori_loop(1, NCOL, s_wait, 0)
+
+    e_stage(0)
 
     def rows_of(z, h, j):
         return (z, pl.ds(128 * h + j, 8, stride=STEP), slice(None))
@@ -286,85 +377,10 @@
     gcoef[grp, 2] = tmp[0, bottom, :]
     gcoef[grp, 3] = tmp[1, bottom, :]
 
-    def g_copy(buf, send, recv, dest, source):
-        return pltpu.make_async_remote_copy(
-            src_ref=buf.at[source],
-            dst_ref=buf.at[source],
-            send_sem=send.at[dest],
-            recv_sem=recv.at[source],
-            device_id={"grp": dest},
-            device_id_type=MESH,
-        )
-
     for o in range(1, NGRP):
         g_copy(gcoef, gc_send, gc_recv, (grp + o) % NGRP, grp).start()
 
-    def e_copy(way, c, dest):
-        rows = pl.ds(pl.multiple_of(c * ZR, ZR), ZR)
-        src, dst = ((eu_out, eu_in), (ed_out, ed_in))[way]
-        return pltpu.make_async_remote_copy(
-            src_ref=src.at[rows],
-            dst_ref=dst.at[rows],
-            send_sem=e_send.at[way, c],
-            recv_sem=e_recv.at[way, c],
-            device_id={"lay": dest},
-            device_id_type=MESH,
-        )
-
-    def q_copy(way, c, dest):
-        rows = pl.ds(pl.multiple_of(c * ZR, ZR), ZR)
-        src, dst = ((qu_out, qu_in), (qd_out, qd_in))[way]
-        return pltpu.make_async_remote_copy(
-            src_ref=src.at[rows],
-            dst_ref=dst.at[rows],
-            send_sem=q_send.at[way, c],
-            recv_sem=q_recv.at[way, c],
-            device_id={"lay": dest},
-            device_id_type=MESH,
-        )
-
-    @pl.when(lay == 0)
-    def _():
-        eu_in[...] = jnp.ones((ROWS, LANES), F32)
-        qu_in[...] = jnp.zeros((ROWS, LANES), F32)
-
-    @pl.when(lay == NLAY - 1)
-    def _():
-        ed_in[...] = jnp.ones((ROWS, LANES), F32)
-        qd_in[...] = jnp.zeros((ROWS, LANES), F32)
-
-    def e_step(t, carry):
-        for way in range(2):
-            back = lay if way == 0 else NLAY - 1 - lay
-            dest = jnp.minimum(lay + 1, NLAY - 1) if way == 0 else jnp.maximum(lay - 1, 0)
-            c = t - back
-
-            @pl.when((c >= 0) & (c < ZCH))
-            def _():
-                rows = pl.ds(pl.multiple_of(c * ZR, ZR), ZR)
-                src, out, wr, pr = ((eu_in, eu_out, wu, pu), (ed_in, ed_out, wd, pd))[way]
-
-                @pl.when(back > 0)
-                def _():
-                    e_copy(way, c, dest).wait_recv()
-
-                e = src[rows, :]
-                for i in range(L) if way == 0 else range(L - 1, -1, -1):
-                    s = ys[i, rows, :]
-                    se = s * e
-                    w = 1.0 / (1.0 + s + se)
-                    e = (1.0 + se) * w
-                    wr[i, rows, :] = w
-                    pr[i, rows, :] = s * w
-                out[rows, :] = e
-
-                @pl.when(back < NLAY - 1)
-                def _():
-                    e_copy(way, c, dest).start()
-
-        return carry
-
-    lax.fori_loop(0, ZCH + NLAY - 1, e_step, 0)
+    e_stage(1)
 
     for chunk in range(FCH):
 
@@ -393,8 +409,13 @@
     tmp[3] = q + yr[STEP - 1] * f
     gval[grp, 0] = tmp[2, top, :]
     gval[grp, 1] = tmp[3, bottom, :]
+
     for o in range(1, NGRP):
         g_copy(gval, gv_send, gv_recv, (grp + o) % NGRP, grp).start()
+
+    e_stage(2)
+    e_stage(3)
+
     for o in range(1, NGRP):
         g_copy(gcoef, gc_send, gc_recv, grp, (grp + NGRP - o) % NGRP).wait_recv()
     for o in range(1, NGRP):
@@ -444,50 +465,66 @@
                 m = 16 * z + 8 * h
                 sec[rows_of(z, h, j)] = x[m : m + 8]
 
-    def q_step(t, carry):
+    def q_local(c, carry):
+        rows = pl.ds(pl.multiple_of(c * QR, QR), QR)
         for way in range(2):
-            back = lay if way == 0 else NLAY - 1 - lay
-            dest = jnp.minimum(lay + 1, NLAY - 1) if way == 0 else jnp.maximum(lay - 1, 0)
-            c = t - back
-
-            @pl.when((c >= 0) & (c < ZCH))
+            out, wr, pr = ((qu_out, wu, pu), (qd_out, wd, pd))[way]
+            order = list(range(L) if way == 0 else range(L - 1, -1, -1))
+            q = sec[order[0], rows, :] * wr[order[0], rows, :]
+            for i in order[1:]:
+                q = sec[i, rows, :] * wr[i, rows, :] + pr[i, rows, :] * q
+            out[rows, :] = q
+        for k in range(NLAY):
+
+            @pl.when(lay == k)
             def _():
-                rows = pl.ds(pl.multiple_of(c * ZR, ZR), ZR)
-                src, out, wr, pr = ((qu_in, qu_out, wu, pu), (qd_in, qd_out, wd, pd))[way]
-                order = range(L) if way == 0 else range(L - 1, -1, -1)
-
-                @pl.when(back > 0)
-                def _():
-                    q_copy(way, c, dest).wait_recv()
-
-                q = src[rows, :]
-                for i in order:
-                    q = sec[i, rows, :] * wr[i, rows, :] + pr[i, rows, :] * q
-                    if way == 0:
-                        res[i, rows, :] = q
-                out[rows, :] = q
-
-                @pl.when(back < NLAY - 1)
-                def _():
-                    q_copy(way, c, dest).start()
-
-        c = t - jnp.maximum(lay, NLAY - 1 - lay)
-
-        @pl.when((c >= 0) & (c < ZCH))
+                for way in range(2):
+                    for dest in reversed(ahead(way, k)):
+                        q_copy(way, c, dest, k).start()
+
+        return carry
+
+    lax.fori_loop(0, QCH, q_local, 0)
+
+    for k in range(NLAY):
+
+        @pl.when(lay == k)
         def _():
-            rows = pl.ds(pl.multiple_of(c * ZR, ZR), ZR)
-            ep = eu_out[rows, :]
-            p = 1.0 - ep
-            x = (res[L - 1, rows, :] + p * qd_in[rows, :]) / (ep + p * ed_in[rows, :])
-            res[L - 1, rows, :] = x
-            for i in range(L - 2, -1, -1):
-                x = res[i, rows, :] + pu[i, rows, :] * x
-                res[i, rows, :] = x
-            pltpu.make_async_copy(res.at[:, rows, :], out_hbm.at[:, rows, :], out_sem.at[c]).start()
-
-        return carry
-
-    lax.fori_loop(0, ZCH + NLAY - 1, q_step, 0)
+            for source in (1, 2):
+                if source != k:
+                    r_copy(0, k, source).wait_recv()
+
+            def finish(c, carry):
+                rows = pl.ds(pl.multiple_of(c * QR, QR), QR)
+                for source in range(NLAY):
+                    if source != k:
+                        q_copy(0, c, k, source).wait_recv()
+                behind = []
+                for way in range(2):
+                    order = range(k) if way == 0 else range(NLAY - 1, k, -1)
+                    q = None
+                    for source in order:
+                        q = q_in[source, rows, :] + (0.0 if q is None else r_in[source, rows, :] * q)
+                    behind.append(q)
+                q, after_q = behind
+                q_all = []
+                for i in range(L):
+                    own = sec[i, rows, :] * wu[i, rows, :]
+                    q = own if q is None else own + pu[i, rows, :] * q
+                    q_all.append(q)
+                x = q
+                if after_q is not None:
+                    ep = eu_out[rows, :]
+                    p = 1.0 - ep
+                    x = (q + p * after_q) / (ep + p * ed_in[rows, :])
+                res[L - 1, rows, :] = x
+                for i in range(L - 2, -1, -1):
+                    x = q_all[i] + pu[i, rows, :] * x
+                    res[i, rows, :] = x
+                out_copy(c).start()
+                return carry
+
+            lax.fori_loop(0, QCH, finish, 0)
 
     def s_done(o, carry):
         s_copy((col + o) % NCOL, col).wait_send()
@@ -499,20 +536,22 @@
     for o in range(1, NGRP):
         g_copy(gcoef, gc_send, gc_recv, (grp + o) % NGRP, grp).wait_send()
         g_copy(gval, gv_send, gv_recv, (grp + o) % NGRP, grp).wait_send()
-    for c in range(ZCH):
-
-        @pl.when(lay < NLAY - 1)
+    for k in range(NLAY):
+
+        @pl.when(lay == k)
         def _():
-            e_copy(0, c, jnp.minimum(lay + 1, NLAY - 1)).wait_send()
-            q_copy(0, c, jnp.minimum(lay + 1, NLAY - 1)).wait_send()
-
-        @pl.when(lay > 0)
-        def _():
-            e_copy(1, c, jnp.maximum(lay - 1, 0)).wait_send()
-            q_copy(1, c, jnp.maximum(lay - 1, 0)).wait_send()
-
-        rows = pl.ds(c * ZR, ZR)
-        pltpu.make_async_copy(res.at[:, rows, :], out_hbm.at[:, rows, :], out_sem.at[c]).wait()
+            for way in range(2):
+                for dest in ahead(way, k):
+                    if abs(dest - k) == 1:
+                        for c in range(ZCH):
+                            e_copy(way, c, dest).wait_send()
+                    if k in (1, 2):
+                        r_copy(way, dest, k).wait_send()
+                    for c in range(QCH):
+                        q_copy(way, c, dest, k).wait_send()
+
+    for c in range(QCH):
+        out_copy(c).wait()
 
 
 def per_device(salinity, zone_ids, flow_speed, fixed_cells, dispersivity):
@@ -540,11 +579,11 @@
             vm((5, LINES, LANES)), vm((5, LINES, LANES)), vm((4, LINES, LANES)), vm((4, LINES, LANES)),
             vm((NGRP, 4, L, LANES)), vm((NGRP, 2, L, LANES)),
             vm(slab), vm(slab), vm(slab), vm(slab), vm(slab),
-            vm(plane), vm(plane), vm(plane), vm(plane), vm(plane), vm(plane), vm(plane), vm(plane),
-            vm(slab),
+            vm(plane), vm(plane), vm(plane), vm(plane), vm(plane), vm(plane), vm((NLAY,) + plane),
+            vm(plane), vm(plane), vm((NLAY,) + plane), vm(slab),
             dma((4,)), dma((NCOL,)), dma((NCOL,)), dma((FCH, NCOL)), dma((FCH, NCOL)),
             dma((NGRP,)), dma((NGRP,)), dma((NGRP,)), dma((NGRP,)),
-            dma((2, ZCH)), dma((2, ZCH)), dma((2, ZCH)), dma((2, ZCH)), dma((ZCH,)),
+            dma((2, ZCH)), dma((2, ZCH)), dma((NLAY,)), dma((NLAY,)), dma((QCH, NLAY)), dma((QCH, NLAY)), dma((QCH,)),
         ],
         compiler_params=pltpu.CompilerParams(
             collective_id=0, has_side_effects=True, vmem_limit_bytes=56 * 1024 * 1024

time: 62.7 us -> 46.5 us (0.74)
  the two profiles are of different devices: /device:TPU:32 before, /device:TPU:1 now
where the time goes in v2:
time: 46.5 us; the launch traced here: 46.3 us
  Pallas kernels  44.4 us (95%)
  local copies, waits for them, and re-layouts  1.87 us (4%)
    pallas_call x1, Pallas kernels, per_device(): pl.pallas_call(kernel, out_shape=jax.ShapeDtypeStruct(slab, F32), in_spec...  44.4 us
    unnamed x1, local copies, waits for them, and re-layouts  1.87 us

profile of v2, /device:TPU:1, one launch (start us, length us, event | category | flops | bytes accessed | tf_op | source)
XLA Modules:
  0.0 46.3 jit_solution(7058139467140273384)
XLA Ops:
  0.0 44.4 %lod_step.1 = f32[4,256,128]{2,1,0:T(8,128)} custom-call(f32[4,16,2048]{2,1,0:T(8,128)} %sal_hbm.1, s32[4,16,2048]{2,1,0:T(8,128)} %zone_hbm.1, f32[4,16,2048]{2,1,0:T(8,128)} %flow_hbm.1, s32[4,16,2048]{2,1,0:T(8,128)} %fixed_hbm.1, f32[2,8]{1,0:T(2,128)} %disp_ref.1), custom_call_target="tpu_custom_call" | custom-call | tf_op jit(solution)/shard_map/lod_step/pallas_call | solution.py:569
  44.4 1.9 %copy.7 = f32[4,256,128]{2,1,0:T(8,128)} copy(f32[4,256,128]{2,1,0:T(8,128)} %lod_step.1) | data formatting | bytes 1048576

commit v3 on v2

--- a/solution.py
+++ b/solution.py
@@ -16,10 +16,8 @@
 ROWS = NCOL * RB
 ZCH = 4
 ZR = ROWS // ZCH
-QCH = 2
+QCH = 4
 QR = ROWS // QCH
-FCH = 2
-FL = L // FCH
 MESH = pl.DeviceIdType.MESH
 F32 = jnp.float32
 
@@ -48,12 +46,12 @@
 def kernel(
     sal_hbm, zone_hbm, flow_hbm, fixed_hbm, disp_ref, out_hbm,
     sal, zone, flow, fixed,
-    long_nat, st, ft, ys, yf,
+    long_nat, st, ft, ct, ys, yf, cy, yb, yc,
     us, uf, up, uq, ur,
     yd, yfd, yp, yw, yr, lev_a, lev_c, lev_i, tmp,
     gcoef, gval,
     sec, wu, pu, wd, pd, eu_in, ed_in, eu_out, ed_out, ru, rd, r_in, qu_out, qd_out, q_in, res,
-    in_sem, s_send, s_recv, f_send, f_recv, gc_send, gc_recv, gv_send, gv_recv,
+    in_sem, s_send, s_recv, c_send, c_recv, f_send, f_recv, gc_send, gc_recv, gv_send, gv_recv,
     e_send, e_recv, r_send, r_recv, q_send, q_recv, out_sem,
 ):
     grp = lax.axis_index("grp")
@@ -70,12 +68,22 @@
             device_id_type=MESH,
         )
 
-    def f_copy(chunk, dest, source):
+    def f_copy(dest, source):
         return pltpu.make_async_remote_copy(
-            src_ref=ft.at[dest, pl.ds(chunk * FL, FL)],
-            dst_ref=yf.at[pl.ds(chunk * FL, FL), pl.ds(source * RB, RB), :],
-            send_sem=f_send.at[chunk, dest],
-            recv_sem=f_recv.at[chunk, source],
+            src_ref=ft.at[dest],
+            dst_ref=yf.at[:, pl.ds(source * RB, RB), :],
+            send_sem=f_send.at[dest],
+            recv_sem=f_recv.at[source],
+            device_id={"col": dest},
+            device_id_type=MESH,
+        )
+
+    def c_copy(dest, source):
+        return pltpu.make_async_remote_copy(
+            src_ref=ct.at[dest],
+            dst_ref=cy.at[source],
+            send_sem=c_send.at[dest],
+            recv_sem=c_recv.at[source],
             device_id={"col": dest},
             device_id_type=MESH,
         )
@@ -102,12 +110,12 @@
             device_id_type=MESH,
         )
 
-    def r_copy(way, dest, source):
+    def r_copy(way, dest):
         return pltpu.make_async_remote_copy(
             src_ref=(ru, rd)[way],
-            dst_ref=r_in.at[source],
-            send_sem=r_send.at[dest],
-            recv_sem=r_recv.at[source],
+            dst_ref=r_in,
+            send_sem=r_send.at[0],
+            recv_sem=r_recv.at[0],
             device_id={"lay": dest},
             device_id_type=MESH,
         )
@@ -129,6 +137,31 @@
 
     def ahead(way, k):
         return range(k + 1, NLAY) if way == 0 else range(k - 1, -1, -1)
+
+    whole = (LINES, LANES)
+
+    def to_steps(flat, steps_ref):
+        for m in range(LINES // 8):
+            for j in range(STEP):
+                steps_ref[j, pl.ds(8 * m, 8), :] = flat[pl.ds(8 * STEP * m + j, 8, stride=STEP), :]
+
+    def block_factors(steps_ref, w_ref, p_ref, r_ref):
+        e = jnp.ones(whole, F32)
+        r = jnp.ones(whole, F32)
+        eb = jnp.ones(whole, F32)
+        for j in range(1, STEP):
+            s = steps_ref[j]
+            se = s * e
+            w = 1.0 / (1.0 + s + se)
+            p = s * w
+            e = (1.0 + se) * w
+            r_now = r * p
+            eb = eb - r * r_now
+            r = r_now
+            w_ref[j] = w
+            p_ref[j] = p
+            r_ref[j] = r
+        return e, r, eb
 
     def e_stage(k):
         for way in range(2):
@@ -162,9 +195,8 @@
                     return carry
 
                 lax.fori_loop(0, ZCH, step, 0)
-                if 0 < k < NLAY - 1:
-                    for dest in ahead(way, me):
-                        r_copy(way, dest, me).start()
+                if k == 1:
+                    r_copy(way, ahead(way, me)[0]).start()
 
     loads = [
         pltpu.make_async_copy(zone_hbm, zone, in_sem.at[0]),
@@ -184,7 +216,7 @@
     lax.fori_loop(1, NCOL, greet_col, 0)
     for o in range(1, NGRP):
         pl.semaphore_signal(barrier, inc=1, device_id={"grp": (grp + o) % NGRP}, device_id_type=MESH)
-    for o in (1, NLAY - 1):
+    for o in range(1, NLAY):
         pl.semaphore_signal(barrier, inc=1, device_id={"lay": (lay + o) % NLAY}, device_id_type=MESH)
 
     lane = lax.broadcasted_iota(jnp.int32, (8, LANES), 1)
@@ -208,7 +240,7 @@
 
     lax.fori_loop(0, L, couple, 0)
 
-    pl.semaphore_wait(barrier, NCOL - 1 + NGRP - 1 + 2)
+    pl.semaphore_wait(barrier, NCOL - 1 + NGRP - 1 + NLAY - 1)
 
     def s_start(o, carry):
         s_copy((col + o) % NCOL, col).start()
@@ -216,6 +248,9 @@
 
     lax.fori_loop(1, NCOL, s_start, 0)
     ys[:, pl.ds(col * RB, RB), :] = st[col]
+
+    to_steps(st.reshape(NCOL * LINES, LANES), yd)
+    block_factors(yd, yw, yp, yr)
 
     loads[3].wait()
 
@@ -233,7 +268,6 @@
 
     lax.fori_loop(0, L, spread, 0)
 
-    whole = (LINES, LANES)
     e = jnp.ones(whole, F32)
     r = jnp.ones(whole, F32)
     q = jnp.zeros(whole, F32)
@@ -294,26 +328,53 @@
         x = uq[j] + ur[j] * f + up[j] * x
         uf[j] = x
 
-    for chunk in range(FCH):
-
-        def gather(z, carry):
-            for half in range(2):
-                rows = pl.ds(8 * half, 8)
-                line = pl.ds(pl.multiple_of(z * RB + 8 * half, 8), 8)
-                parts = butterfly([uf[j, line, :] for j in range(STEP)], lane)
-                for b in range(NCOL):
-                    ft[b, z, rows, :] = parts[b]
-            return carry
-
-        lax.fori_loop(chunk * FL, (chunk + 1) * FL, gather, 0)
-
-        def f_start(o, carry):
-            f_copy(chunk, (col + o) % NCOL, col).start()
-            return carry
-
-        lax.fori_loop(1, NCOL, f_start, 0)
-        layers = pl.ds(chunk * FL, FL)
-        yf[layers, pl.ds(col * RB, RB), :] = ft[col, layers]
+    def gather(z, carry):
+        for half in range(2):
+            rows = pl.ds(8 * half, 8)
+            line = pl.ds(pl.multiple_of(z * RB + 8 * half, 8), 8)
+            parts = butterfly([uf[j, line, :] for j in range(STEP)], lane)
+            for b in range(NCOL):
+                ft[b, z, rows, :] = parts[b]
+        return carry
+
+    lax.fori_loop(0, L, gather, 0)
+
+    ft_flat = ft.reshape(NCOL * LINES, LANES)
+    to_steps(ft_flat, yfd)
+    q = yfd[1] * yw[1]
+    yfd[1] = q
+    alpha = q
+    for j in range(2, STEP):
+        q = yfd[j] * yw[j] + yp[j] * q
+        yfd[j] = q
+        alpha = alpha + yr[j - 1] * q
+    head = yfd[0] + yd[0] * alpha
+    for b in range(NCOL):
+        ct[b, 0] = head[L * b : L * (b + 1)]
+        ct[b, 1] = q[L * b : L * (b + 1)]
+
+    def c_start(o, carry):
+        c_copy((col + o) % NCOL, col).start()
+        return carry
+
+    lax.fori_loop(1, NCOL, c_start, 0)
+    cy[col] = ct[col]
+
+    x = yfd[STEP - 1]
+    for j in range(STEP - 1, -1, -1):
+        if j == 0:
+            x = jnp.zeros(whole, F32)
+        elif j < STEP - 1:
+            x = yfd[j] + yp[j] * x
+        for m in range(LINES // 8):
+            ft_flat[pl.ds(8 * STEP * m + j, 8, stride=STEP), :] = x[8 * m : 8 * m + 8]
+
+    def f_start(o, carry):
+        f_copy((col + o) % NCOL, col).start()
+        return carry
+
+    lax.fori_loop(1, NCOL, f_start, 0)
+    yf[:, pl.ds(col * RB, RB), :] = ft[col]
 
     def s_wait(o, carry):
         s_copy(col, (col + NCOL - o) % NCOL).wait_recv()
@@ -323,29 +384,9 @@
 
     e_stage(0)
 
-    def rows_of(z, h, j):
-        return (z, pl.ds(128 * h + j, 8, stride=STEP), slice(None))
-
-    for z in range(L):
-        for h in range(2):
-            for j in range(STEP):
-                yd[j, pl.ds(16 * z + 8 * h, 8), :] = ys[rows_of(z, h, j)]
-
-    e = jnp.ones(whole, F32)
-    r = jnp.ones(whole, F32)
-    eb = jnp.ones(whole, F32)
-    for j in range(1, STEP):
-        s = yd[j]
-        se = s * e
-        w = 1.0 / (1.0 + s + se)
-        p = s * w
-        e = (1.0 + se) * w
-        r_now = r * p
-        eb = eb - r * r_now
-        r = r_now
-        yw[j] = w
-        yp[j] = p
-        yr[j] = r
+    to_steps(ys.reshape(L * ROWS, LANES), yd)
+
+    e, r, eb = block_factors(yd, yw, yp, yr)
     block = lax.broadcasted_iota(jnp.int32, whole, 0) % RB
 
     def above(v, d, edge):
@@ -380,28 +421,32 @@
     for o in range(1, NGRP):
         g_copy(gcoef, gc_send, gc_recv, (grp + o) % NGRP, grp).start()
 
-    e_stage(1)
-
-    for chunk in range(FCH):
-
-        def f_wait(o, carry):
-            f_copy(chunk, col, (col + NCOL - o) % NCOL).wait_recv()
-            return carry
-
-        lax.fori_loop(1, NCOL, f_wait, 0)
-        for z in range(chunk * FL, (chunk + 1) * FL):
-            for h in range(2):
-                for j in range(STEP):
-                    yfd[j, pl.ds(16 * z + 8 * h, 8), :] = yf[rows_of(z, h, j)]
-
-    q = yfd[1] * yw[1]
-    yfd[1] = q
-    alpha = q
-    for j in range(2, STEP):
-        q = yfd[j] * yw[j] + yp[j] * q
-        yfd[j] = q
-        alpha = alpha + yr[j - 1] * q
-    f = (yfd[0] + yd[0] * (above(q, 1, 0.0) + alpha)) * yw[0]
+    to_left = jnp.zeros(whole, F32)
+    to_right = jnp.ones(whole, F32)
+    yb_flat = yb.reshape(L * ROWS, LANES)
+    yc_flat = yc.reshape(L * ROWS, LANES)
+    for j in range(STEP - 1, -1, -1):
+        if j == 0:
+            to_left, to_right = jnp.ones(whole, F32), jnp.zeros(whole, F32)
+        else:
+            to_left = yr[j] + yp[j] * to_left
+            to_right = yp[j] * to_right
+        for m in range(LINES // 8):
+            rows = pl.ds(8 * STEP * m + j, 8, stride=STEP)
+            yb_flat[rows, :] = to_left[8 * m : 8 * m + 8]
+            yc_flat[rows, :] = to_right[8 * m : 8 * m + 8]
+
+    def c_wait(o, carry):
+        c_copy(col, (col + NCOL - o) % NCOL).wait_recv()
+        return carry
+
+    lax.fori_loop(1, NCOL, c_wait, 0)
+    for k in range(NCOL):
+        tmp[2, pl.ds(k, L, stride=NCOL), :] = cy[k, 0]
+        tmp[3, pl.ds(k, L, stride=NCOL), :] = cy[k, 1]
+
+    q = tmp[3]
+    f = (tmp[2] + yd[0] * above(q, 1, 0.0)) * yw[0]
     for m in range(4):
         d = 1 << m
         f = f * lev_i[m] + lev_a[m] * above(f, d, 0.0) + lev_c[m] * below(f, d, 0.0)
@@ -413,8 +458,7 @@
     for o in range(1, NGRP):
         g_copy(gval, gv_send, gv_recv, (grp + o) % NGRP, grp).start()
 
-    e_stage(2)
-    e_stage(3)
+    e_stage(1)
 
     for o in range(1, NGRP):
         g_copy(gcoef, gc_send, gc_recv, grp, (grp + NGRP - o) % NGRP).wait_recv()
@@ -454,69 +498,95 @@
 
     right = per_line(right)
     f = f + lev_a[4] * per_line(left) + lev_c[4] * right
-    x = jnp.where(block == RB - 1, right, pltpu.roll(f, LINES - 1, 0))
-    for j in range(STEP - 1, -1, -1):
-        if j == 0:
-            x = f
-        else:
-            x = yfd[j] + yr[j] * f + yp[j] * x
-        for z in range(L):
-            for h in range(2):
-                m = 16 * z + 8 * h
-                sec[rows_of(z, h, j)] = x[m : m + 8]
-
-    def q_local(c, carry):
-        rows = pl.ds(pl.multiple_of(c * QR, QR), QR)
-        for way in range(2):
+    tmp[2] = f
+    tmp[3] = jnp.where(block == RB - 1, right, pltpu.roll(f, LINES - 1, 0))
+
+    def f_wait(o, carry):
+        f_copy(col, (col + NCOL - o) % NCOL).wait_recv()
+        return carry
+
+    lax.fori_loop(1, NCOL, f_wait, 0)
+
+    def fill(z, carry):
+        for k in range(NCOL):
+            rows = pl.ds(RB * k, RB)
+            here = tmp[2, pl.ds(z * NCOL + k, 1), :]
+            there = tmp[3, pl.ds(z * NCOL + k, 1), :]
+            sec[z, rows, :] = yf[z, rows, :] + yb[z, rows, :] * here + yc[z, rows, :] * there
+        return carry
+
+    lax.fori_loop(0, L, fill, 0)
+
+    for k in range(NLAY):
+
+        @pl.when(lay == k)
+        def _():
+            way = 0 if k < 2 else 1
             out, wr, pr = ((qu_out, wu, pu), (qd_out, wd, pd))[way]
             order = list(range(L) if way == 0 else range(L - 1, -1, -1))
-            q = sec[order[0], rows, :] * wr[order[0], rows, :]
-            for i in order[1:]:
-                q = sec[i, rows, :] * wr[i, rows, :] + pr[i, rows, :] * q
-            out[rows, :] = q
-        for k in range(NLAY):
-
-            @pl.when(lay == k)
-            def _():
-                for way in range(2):
-                    for dest in reversed(ahead(way, k)):
-                        q_copy(way, c, dest, k).start()
-
-        return carry
-
-    lax.fori_loop(0, QCH, q_local, 0)
-
-    for k in range(NLAY):
+            dests = [ahead(way, k)[1], ahead(way, k)[0]] if k in (0, NLAY - 1) else [ahead(way, k)[0]]
+
+            def q_local(c, carry):
+                rows = pl.ds(pl.multiple_of(c * QR, QR), QR)
+                q = sec[order[0], rows, :] * wr[order[0], rows, :]
+                for i in order[1:]:
+                    q = sec[i, rows, :] * wr[i, rows, :] + pr[i, rows, :] * q
+                out[rows, :] = q
+                for dest in dests:
+                    q_copy(way, c, dest, k).start()
+                return carry
+
+            lax.fori_loop(0, QCH, q_local, 0)
+
+    e_stage(2)
+    for k in (1, 2):
 
         @pl.when(lay == k)
         def _():
-            for source in (1, 2):
-                if source != k:
-                    r_copy(0, k, source).wait_recv()
+            way = 0 if k == 2 else 1
+            out, wr, pr = ((qu_out, wu, pu), (qd_out, wd, pd))[way]
+            order = list(range(L) if way == 0 else range(L - 1, -1, -1))
+            near, far = (k - 1, k - 2) if way == 0 else (k + 1, k + 2)
+            r_copy(way, k).wait_recv()
+
+            def q_middle(c, carry):
+                rows = pl.ds(pl.multiple_of(c * QR, QR), QR)
+                q_copy(0, c, k, near).wait_recv()
+                q_copy(0, c, k, far).wait_recv()
+                q = q_in[near, rows, :] + r_in[rows, :] * q_in[far, rows, :]
+                q_in[far, rows, :] = q
+                for i in order:
+                    q = sec[i, rows, :] * wr[i, rows, :] + pr[i, rows, :] * q
+                out[rows, :] = q
+                q_copy(way, c, ahead(way, k)[0], k).start()
+                return carry
+
+            lax.fori_loop(0, QCH, q_middle, 0)
+
+    e_stage(3)
+
+    for k in range(NLAY):
+
+        @pl.when(lay == k)
+        def _():
+            below_from = {0: None, 1: 0, 2: 0, 3: 2}[k]
+            above_from = {0: 1, 1: 3, 2: 3, 3: None}[k]
 
             def finish(c, carry):
                 rows = pl.ds(pl.multiple_of(c * QR, QR), QR)
-                for source in range(NLAY):
-                    if source != k:
-                        q_copy(0, c, k, source).wait_recv()
-                behind = []
-                for way in range(2):
-                    order = range(k) if way == 0 else range(NLAY - 1, k, -1)
-                    q = None
-                    for source in order:
-                        q = q_in[source, rows, :] + (0.0 if q is None else r_in[source, rows, :] * q)
-                    behind.append(q)
-                q, after_q = behind
+                own = {0: 1, 1: 0, 2: 3, 3: 2}[k]
+                q_copy(0, c, k, own).wait_recv()
+                q = None if below_from is None else q_in[below_from, rows, :]
                 q_all = []
                 for i in range(L):
-                    own = sec[i, rows, :] * wu[i, rows, :]
-                    q = own if q is None else own + pu[i, rows, :] * q
+                    mine = sec[i, rows, :] * wu[i, rows, :]
+                    q = mine if q is None else mine + pu[i, rows, :] * q
                     q_all.append(q)
                 x = q
-                if after_q is not None:
+                if above_from is not None:
                     ep = eu_out[rows, :]
                     p = 1.0 - ep
-                    x = (q + p * after_q) / (ep + p * ed_in[rows, :])
+                    x = (q + p * q_in[above_from, rows, :]) / (ep + p * ed_in[rows, :])
                 res[L - 1, rows, :] = x
                 for i in range(L - 2, -1, -1):
                     x = q_all[i] + pu[i, rows, :] * x
@@ -528,8 +598,8 @@
 
     def s_done(o, carry):
         s_copy((col + o) % NCOL, col).wait_send()
-        for chunk in range(FCH):
-            f_copy(chunk, (col + o) % NCOL, col).wait_send()
+        c_copy((col + o) % NCOL, col).wait_send()
+        f_copy((col + o) % NCOL, col).wait_send()
         return carry
 
     lax.fori_loop(1, NCOL, s_done, 0)
@@ -541,14 +611,18 @@
         @pl.when(lay == k)
         def _():
             for way in range(2):
-                for dest in ahead(way, k):
-                    if abs(dest - k) == 1:
-                        for c in range(ZCH):
-                            e_copy(way, c, dest).wait_send()
-                    if k in (1, 2):
-                        r_copy(way, dest, k).wait_send()
-                    for c in range(QCH):
-                        q_copy(way, c, dest, k).wait_send()
+                back = k if way == 0 else NLAY - 1 - k
+                if back == NLAY - 1:
+                    continue
+                dest = ahead(way, k)[0]
+                for c in range(ZCH):
+                    e_copy(way, c, dest).wait_send()
+                if back == 1:
+                    r_copy(way, dest).wait_send()
+                for c in range(QCH):
+                    q_copy(way, c, dest, k).wait_send()
+                    if back == 0:
+                        q_copy(way, c, ahead(way, k)[1], k).wait_send()
 
     for c in range(QCH):
         out_copy(c).wait()
@@ -573,17 +647,18 @@
         out_specs=hbm,
         scratch_shapes=[
             vm(nat), vm(nat, jnp.int32), vm(nat), vm(nat, jnp.int32),
-            vm(by_dest), vm(by_dest), vm(by_dest), vm(slab), vm(slab),
+            vm(by_dest), vm(by_dest), vm(by_dest), vm((NCOL, 2, L, LANES)), vm(slab), vm(slab),
+            vm((NCOL, 2, L, LANES)), vm(slab), vm(slab),
             vm(steps), vm(steps), vm(steps), vm(steps), vm(steps),
             vm(steps), vm(steps), vm(steps), vm(steps), vm(steps),
             vm((5, LINES, LANES)), vm((5, LINES, LANES)), vm((4, LINES, LANES)), vm((4, LINES, LANES)),
             vm((NGRP, 4, L, LANES)), vm((NGRP, 2, L, LANES)),
             vm(slab), vm(slab), vm(slab), vm(slab), vm(slab),
-            vm(plane), vm(plane), vm(plane), vm(plane), vm(plane), vm(plane), vm((NLAY,) + plane),
+            vm(plane), vm(plane), vm(plane), vm(plane), vm(plane), vm(plane), vm(plane),
             vm(plane), vm(plane), vm((NLAY,) + plane), vm(slab),
-            dma((4,)), dma((NCOL,)), dma((NCOL,)), dma((FCH, NCOL)), dma((FCH, NCOL)),
+            dma((4,)), dma((NCOL,)), dma((NCOL,)), dma((NCOL,)), dma((NCOL,)), dma((NCOL,)), dma((NCOL,)),
             dma((NGRP,)), dma((NGRP,)), dma((NGRP,)), dma((NGRP,)),
-            dma((2, ZCH)), dma((2, ZCH)), dma((NLAY,)), dma((NLAY,)), dma((QCH, NLAY)), dma((QCH, NLAY)), dma((QCH,)),
+            dma((2, ZCH)), dma((2, ZCH)), dma((1,)), dma((1,)), dma((QCH, NLAY)), dma((QCH, NLAY)), dma((QCH,)),
         ],
         compiler_params=pltpu.CompilerParams(
             collective_id=0, has_side_effects=True, vmem_limit_bytes=56 * 1024 * 1024

time: 46.5 us -> 43.3 us (0.931)
  Pallas kernels: 44.4 us -> 41.2 us
    pallas_call x1, Pallas kernels: 44.4 us -> 41.2 us  [per_device(): pl.pallas_call(kernel, out_shape=jax.ShapeDtypeStruct(slab, F32), in_spec...]
where the time goes in v3:
time: 43.3 us; the launch traced here: 43.1 us
  Pallas kernels  41.2 us (95%)
  local copies, waits for them, and re-layouts  1.87 us (4%)
    pallas_call x1, Pallas kernels, per_device(): pl.pallas_call(kernel, out_shape=jax.ShapeDtypeStruct(slab, F32), in_spec...  41.2 us
    unnamed x1, local copies, waits for them, and re-layouts  1.87 us

profile of v3, /device:TPU:1, one launch (start us, length us, event | category | flops | bytes accessed | tf_op | source)
XLA Modules:
  0.0 43.1 jit_solution(1367109685147529571)
XLA Ops:
  0.0 41.2 %lod_step.1 = f32[4,256,128]{2,1,0:T(8,128)} custom-call(f32[4,16,2048]{2,1,0:T(8,128)} %sal_hbm.1, s32[4,16,2048]{2,1,0:T(8,128)} %zone_hbm.1, f32[4,16,2048]{2,1,0:T(8,128)} %flow_hbm.1, s32[4,16,2048]{2,1,0:T(8,128)} %fixed_hbm.1, f32[2,8]{1,0:T(2,128)} %disp_ref.1), custom_call_target="tpu_custom_call" | custom-call | tf_op jit(solution)/shard_map/lod_step/pallas_call | solution.py:643
  41.2 1.9 %copy.7 = f32[4,256,128]{2,1,0:T(8,128)} copy(f32[4,256,128]{2,1,0:T(8,128)} %lod_step.1) | data formatting | bytes 1048576

commit v4 on v3

--- a/solution.py
+++ b/solution.py
@@ -195,8 +195,6 @@
                     return carry
 
                 lax.fori_loop(0, ZCH, step, 0)
-                if k == 1:
-                    r_copy(way, ahead(way, me)[0]).start()
 
     loads = [
         pltpu.make_async_copy(zone_hbm, zone, in_sem.at[0]),
@@ -517,51 +515,37 @@
 
     lax.fori_loop(0, L, fill, 0)
 
-    for k in range(NLAY):
+    def q_pass(k, way, back):
+        out, wr, pr = ((qu_out, wu, pu), (qd_out, wd, pd))[way]
+        order = list(range(L) if way == 0 else range(L - 1, -1, -1))
+        behind = k - 1 if way == 0 else k + 1
+
+        def step(c, carry):
+            rows = pl.ds(pl.multiple_of(c * QR, QR), QR)
+            if back > 0:
+                q_copy(0, c, k, behind).wait_recv()
+                q = q_in[behind, rows, :]
+            for i in order:
+                mine = sec[i, rows, :] * wr[i, rows, :]
+                q = mine if (back == 0 and i == order[0]) else mine + pr[i, rows, :] * q
+            out[rows, :] = q
+            q_copy(way, c, ahead(way, k)[0], k).start()
+            return carry
+
+        lax.fori_loop(0, QCH, step, 0)
+
+    for k, way, back in ((0, 0, 0), (1, 0, 1), (2, 1, 1), (3, 1, 0)):
 
         @pl.when(lay == k)
         def _():
-            way = 0 if k < 2 else 1
-            out, wr, pr = ((qu_out, wu, pu), (qd_out, wd, pd))[way]
-            order = list(range(L) if way == 0 else range(L - 1, -1, -1))
-            dests = [ahead(way, k)[1], ahead(way, k)[0]] if k in (0, NLAY - 1) else [ahead(way, k)[0]]
-
-            def q_local(c, carry):
-                rows = pl.ds(pl.multiple_of(c * QR, QR), QR)
-                q = sec[order[0], rows, :] * wr[order[0], rows, :]
-                for i in order[1:]:
-                    q = sec[i, rows, :] * wr[i, rows, :] + pr[i, rows, :] * q
-                out[rows, :] = q
-                for dest in dests:
-                    q_copy(way, c, dest, k).start()
-                return carry
-
-            lax.fori_loop(0, QCH, q_local, 0)
+            q_pass(k, way, back)
 
     e_stage(2)
-    for k in (1, 2):
+    for k, way in ((1, 1), (2, 0)):
 
         @pl.when(lay == k)
         def _():
-            way = 0 if k == 2 else 1
-            out, wr, pr = ((qu_out, wu, pu), (qd_out, wd, pd))[way]
-            order = list(range(L) if way == 0 else range(L - 1, -1, -1))
-            near, far = (k - 1, k - 2) if way == 0 else (k + 1, k + 2)
-            r_copy(way, k).wait_recv()
-
-            def q_middle(c, carry):
-                rows = pl.ds(pl.multiple_of(c * QR, QR), QR)
-                q_copy(0, c, k, near).wait_recv()
-                q_copy(0, c, k, far).wait_recv()
-                q = q_in[near, rows, :] + r_in[rows, :] * q_in[far, rows, :]
-                q_in[far, rows, :] = q
-                for i in order:
-                    q = sec[i, rows, :] * wr[i, rows, :] + pr[i, rows, :] * q
-                out[rows, :] = q
-                q_copy(way, c, ahead(way, k)[0], k).start()
-                return carry
-
-            lax.fori_loop(0, QCH, q_middle, 0)
+            q_pass(k, way, 2)
 
     e_stage(3)
 
@@ -569,13 +553,13 @@
 
         @pl.when(lay == k)
         def _():
-            below_from = {0: None, 1: 0, 2: 0, 3: 2}[k]
-            above_from = {0: 1, 1: 3, 2: 3, 3: None}[k]
+            below_from = {0: None, 1: 0, 2: 1, 3: 2}[k]
+            above_from = {0: 1, 1: 2, 2: 3, 3: None}[k]
 
             def finish(c, carry):
                 rows = pl.ds(pl.multiple_of(c * QR, QR), QR)
-                own = {0: 1, 1: 0, 2: 3, 3: 2}[k]
-                q_copy(0, c, k, own).wait_recv()
+                if k in (0, NLAY - 1):
+                    q_copy(0, c, k, 1 if k == 0 else 2).wait_recv()
                 q = None if below_from is None else q_in[below_from, rows, :]
                 q_all = []
                 for i in range(L):
@@ -617,12 +601,8 @@
                 dest = ahead(way, k)[0]
                 for c in range(ZCH):
                     e_copy(way, c, dest).wait_send()
-                if back == 1:
-                    r_copy(way, dest).wait_send()
                 for c in range(QCH):
                     q_copy(way, c, dest, k).wait_send()
-                    if back == 0:
-                        q_copy(way, c, ahead(way, k)[1], k).wait_send()
 
     for c in range(QCH):
         out_copy(c).wait()

time: 43.3 us -> 40.4 us (0.933)
  Pallas kernels: 41.2 us -> 38.3 us
    pallas_call x1, Pallas kernels: 41.2 us -> 38.3 us  [per_device(): pl.pallas_call(kernel, out_shape=jax.ShapeDtypeStruct(slab, F32), in_spec...]
where the time goes in v4:
time: 40.4 us; the launch traced here: 40.2 us
  Pallas kernels  38.3 us (95%)
  local copies, waits for them, and re-layouts  1.87 us (5%)
    pallas_call x1, Pallas kernels, per_device(): pl.pallas_call(kernel, out_shape=jax.ShapeDtypeStruct(slab, F32), in_spec...  38.3 us
    unnamed x1, local copies, waits for them, and re-layouts  1.87 us

profile of v4, /device:TPU:1, one launch (start us, length us, event | category | flops | bytes accessed | tf_op | source)
XLA Modules:
  0.0 40.2 jit_solution(4431317095088325415)
XLA Ops:
  0.0 38.3 %lod_step.1 = f32[4,256,128]{2,1,0:T(8,128)} custom-call(f32[4,16,2048]{2,1,0:T(8,128)} %sal_hbm.1, s32[4,16,2048]{2,1,0:T(8,128)} %zone_hbm.1, f32[4,16,2048]{2,1,0:T(8,128)} %flow_hbm.1, s32[4,16,2048]{2,1,0:T(8,128)} %fixed_hbm.1, f32[2,8]{1,0:T(2,128)} %disp_ref.1), custom_call_target="tpu_custom_call" | custom-call | tf_op jit(solution)/shard_map/lod_step/pallas_call | solution.py:623
  38.3 1.9 %copy.7 = f32[4,256,128]{2,1,0:T(8,128)} copy(f32[4,256,128]{2,1,0:T(8,128)} %lod_step.1) | data formatting | bytes 1048576

commit v5 on v4

--- a/solution.py
+++ b/solution.py
@@ -348,8 +348,8 @@
         alpha = alpha + yr[j - 1] * q
     head = yfd[0] + yd[0] * alpha
     for b in range(NCOL):
-        ct[b, 0] = head[L * b : L * (b + 1)]
-        ct[b, 1] = q[L * b : L * (b + 1)]
+        ct[b, 0:L] = head[L * b : L * (b + 1)]
+        ct[b, L : 2 * L] = q[L * b : L * (b + 1)]
 
     def c_start(o, carry):
         c_copy((col + o) % NCOL, col).start()
@@ -379,8 +379,6 @@
         return carry
 
     lax.fori_loop(1, NCOL, s_wait, 0)
-
-    e_stage(0)
 
     to_steps(ys.reshape(L * ROWS, LANES), yd)
 
@@ -411,13 +409,37 @@
     bottom = pl.ds(RB - 1, L, stride=RB)
     tmp[0] = r * a
     tmp[1] = (1.0 - e) + r * c
-    gcoef[grp, 0] = lev_a[4, top, :]
-    gcoef[grp, 1] = lev_c[4, top, :]
-    gcoef[grp, 2] = tmp[0, bottom, :]
-    gcoef[grp, 3] = tmp[1, bottom, :]
+    gcoef[grp, 0 * L : 1 * L] = lev_a[4, top, :]
+    gcoef[grp, 1 * L : 2 * L] = lev_c[4, top, :]
+    gcoef[grp, 2 * L : 3 * L] = tmp[0, bottom, :]
+    gcoef[grp, 3 * L : 4 * L] = tmp[1, bottom, :]
 
     for o in range(1, NGRP):
         g_copy(gcoef, gc_send, gc_recv, (grp + o) % NGRP, grp).start()
+
+    e_stage(0)
+
+    def c_wait(o, carry):
+        c_copy(col, (col + NCOL - o) % NCOL).wait_recv()
+        return carry
+
+    lax.fori_loop(1, NCOL, c_wait, 0)
+    for k in range(NCOL):
+        tmp[2, pl.ds(k, L, stride=NCOL), :] = cy[k, 0:L]
+        tmp[3, pl.ds(k, L, stride=NCOL), :] = cy[k, L : 2 * L]
+
+    q = tmp[3]
+    f = (tmp[2] + yd[0] * above(q, 1, 0.0)) * yw[0]
+    for m in range(4):
+        d = 1 << m
+        f = f * lev_i[m] + lev_a[m] * above(f, d, 0.0) + lev_c[m] * below(f, d, 0.0)
+    tmp[2] = f
+    tmp[3] = q + yr[STEP - 1] * f
+    gval[grp, 0 * L : 1 * L] = tmp[2, top, :]
+    gval[grp, 1 * L : 2 * L] = tmp[3, bottom, :]
+
+    for o in range(1, NGRP):
+        g_copy(gval, gv_send, gv_recv, (grp + o) % NGRP, grp).start()
 
     to_left = jnp.zeros(whole, F32)
     to_right = jnp.ones(whole, F32)
@@ -434,28 +456,6 @@
             yb_flat[rows, :] = to_left[8 * m : 8 * m + 8]
             yc_flat[rows, :] = to_right[8 * m : 8 * m + 8]
 
-    def c_wait(o, carry):
-        c_copy(col, (col + NCOL - o) % NCOL).wait_recv()
-        return carry
-
-    lax.fori_loop(1, NCOL, c_wait, 0)
-    for k in range(NCOL):
-        tmp[2, pl.ds(k, L, stride=NCOL), :] = cy[k, 0]
-        tmp[3, pl.ds(k, L, stride=NCOL), :] = cy[k, 1]
-
-    q = tmp[3]
-    f = (tmp[2] + yd[0] * above(q, 1, 0.0)) * yw[0]
-    for m in range(4):
-        d = 1 << m
-        f = f * lev_i[m] + lev_a[m] * above(f, d, 0.0) + lev_c[m] * below(f, d, 0.0)
-    tmp[2] = f
-    tmp[3] = q + yr[STEP - 1] * f
-    gval[grp, 0] = tmp[2, top, :]
-    gval[grp, 1] = tmp[3, bottom, :]
-
-    for o in range(1, NGRP):
-        g_copy(gval, gv_send, gv_recv, (grp + o) % NGRP, grp).start()
-
     e_stage(1)
 
     for o in range(1, NGRP):
@@ -463,12 +463,12 @@
     for o in range(1, NGRP):
         g_copy(gval, gv_send, gv_recv, grp, (grp + NGRP - o) % NGRP).wait_recv()
 
-    be = [gcoef[g, 0] for g in range(NGRP)]
-    ga = [gcoef[g, 1] for g in range(NGRP)]
-    rr = [gcoef[g, 2] for g in range(NGRP)]
-    pp = [gcoef[g, 3] for g in range(NGRP)]
-    al = [gval[g, 0] for g in range(NGRP)]
-    qq = [gval[g, 1] for g in range(NGRP)]
+    be = [gcoef[g, 0 * L : 1 * L] for g in range(NGRP)]
+    ga = [gcoef[g, 1 * L : 2 * L] for g in range(NGRP)]
+    rr = [gcoef[g, 2 * L : 3 * L] for g in range(NGRP)]
+    pp = [gcoef[g, 3 * L : 4 * L] for g in range(NGRP)]
+    al = [gval[g, 0 * L : 1 * L] for g in range(NGRP)]
+    qq = [gval[g, 1 * L : 2 * L] for g in range(NGRP)]
     pre_p, pre_q = [pp[0]], [qq[0]]
     for g in range(1, NGRP - 1):
         t = rr[g] / (1.0 - pre_p[-1] * be[g])
@@ -505,15 +505,12 @@
 
     lax.fori_loop(1, NCOL, f_wait, 0)
 
-    def fill(z, carry):
-        for k in range(NCOL):
-            rows = pl.ds(RB * k, RB)
-            here = tmp[2, pl.ds(z * NCOL + k, 1), :]
-            there = tmp[3, pl.ds(z * NCOL + k, 1), :]
-            sec[z, rows, :] = yf[z, rows, :] + yb[z, rows, :] * here + yc[z, rows, :] * there
-        return carry
-
-    lax.fori_loop(0, L, fill, 0)
+    def fill(c):
+        for z in range(L):
+            for n in range(QR // RB):
+                rows = pl.ds(pl.multiple_of(c * QR + RB * n, RB), RB)
+                line = pl.ds(z * NCOL + c * (QR // RB) + n, 1)
+                sec[z, rows, :] = yf[z, rows, :] + yb[z, rows, :] * tmp[2, line, :] + yc[z, rows, :] * tmp[3, line, :]
 
     def q_pass(k, way, back):
         out, wr, pr = ((qu_out, wu, pu), (qd_out, wd, pd))[way]
@@ -522,6 +519,8 @@
 
         def step(c, carry):
             rows = pl.ds(pl.multiple_of(c * QR, QR), QR)
+            if back < 2:
+                fill(c)
             if back > 0:
                 q_copy(0, c, k, behind).wait_recv()
                 q = q_in[behind, rows, :]
@@ -571,11 +570,10 @@
                     ep = eu_out[rows, :]
                     p = 1.0 - ep
                     x = (q + p * q_in[above_from, rows, :]) / (ep + p * ed_in[rows, :])
-                res[L - 1, rows, :] = x
+                out_hbm[L - 1, rows, :] = x
                 for i in range(L - 2, -1, -1):
                     x = q_all[i] + pu[i, rows, :] * x
-                    res[i, rows, :] = x
-                out_copy(c).start()
+                    out_hbm[i, rows, :] = x
                 return carry
 
             lax.fori_loop(0, QCH, finish, 0)
@@ -604,12 +602,10 @@
                 for c in range(QCH):
                     q_copy(way, c, dest, k).wait_send()
 
-    for c in range(QCH):
-        out_copy(c).wait()
-
 
 def per_device(salinity, zone_ids, flow_speed, fixed_cells, dispersivity):
     hbm = pl.BlockSpec(memory_space=pl.ANY)
+    fixed = pl.BlockSpec(memory_space=pltpu.HBM)
     nat = (L, RB, NCOL * LANES)
     slab = (L, ROWS, LANES)
     by_dest = (NCOL, L, RB, LANES)
@@ -624,15 +620,15 @@
         kernel,
         out_shape=jax.ShapeDtypeStruct(slab, F32),
         in_specs=[hbm, hbm, hbm, hbm, pl.BlockSpec(memory_space=pltpu.SMEM)],
-        out_specs=hbm,
+        out_specs=pl.BlockSpec(memory_space=pltpu.VMEM),
         scratch_shapes=[
             vm(nat), vm(nat, jnp.int32), vm(nat), vm(nat, jnp.int32),
-            vm(by_dest), vm(by_dest), vm(by_dest), vm((NCOL, 2, L, LANES)), vm(slab), vm(slab),
-            vm((NCOL, 2, L, LANES)), vm(slab), vm(slab),
+            vm(by_dest), vm(by_dest), vm(by_dest), vm((NCOL, 2 * L, LANES)), vm(slab), vm(slab),
+            vm((NCOL, 2 * L, LANES)), vm(slab), vm(slab),
             vm(steps), vm(steps), vm(steps), vm(steps), vm(steps),
             vm(steps), vm(steps), vm(steps), vm(steps), vm(steps),
             vm((5, LINES, LANES)), vm((5, LINES, LANES)), vm((4, LINES, LANES)), vm((4, LINES, LANES)),
-            vm((NGRP, 4, L, LANES)), vm((NGRP, 2, L, LANES)),
+            vm((NGRP, 4 * L, LANES)), vm((NGRP, 2 * L, LANES)),
             vm(slab), vm(slab), vm(slab), vm(slab), vm(slab),
             vm(plane), vm(plane), vm(plane), vm(plane), vm(plane), vm(plane), vm(plane),
             vm(plane), vm(plane), vm((NLAY,) + plane), vm(slab),
@@ -641,7 +637,7 @@
             dma((2, ZCH)), dma((2, ZCH)), dma((1,)), dma((1,)), dma((QCH, NLAY)), dma((QCH, NLAY)), dma((QCH,)),
         ],
         compiler_params=pltpu.CompilerParams(
-            collective_id=0, has_side_effects=True, vmem_limit_bytes=56 * 1024 * 1024
+            collective_id=0, has_side_effects=True, vmem_limit_bytes=54272 * 1024
         ),
         name="lod_step",
     )(salinity, zone_ids, flow_speed, fixed_cells, dispersivity)

time: 40.4 us -> 39.3 us (0.973)
  Pallas kernels: 38.3 us -> 37.7 us
    pallas_call x1, Pallas kernels: 38.3 us -> 37.7 us  [per_device(): pl.pallas_call(kernel, out_shape=jax.ShapeDtypeStruct(slab, F32), in_spec...]
    unnamed x1 -> x3, local copies, waits for them, and re-layouts: 1.87 us -> 1.47 us
where the time goes in v5:
time: 39.3 us; the launch traced here: 39.2 us
  Pallas kernels  37.7 us (96%)
  local copies, waits for them, and re-layouts  1.47 us (4%)
    pallas_call x1, Pallas kernels, per_device(): pl.pallas_call(kernel, out_shape=jax.ShapeDtypeStruct(slab, F32), in_spec...  37.7 us
    unnamed x3, local copies, waits for them, and re-layouts  1.47 us

profile of v5, /device:TPU:1, one launch (start us, length us, event | category | flops | bytes accessed | tf_op | source)
XLA Modules:
  0.0 39.2 jit_solution(18155791682382053183)
XLA Ops:
  0.0 0.0 copy-start
  0.0 0.7 %copy-done = f32[2,8]{1,0:T(2,128)S(1)} copy-done((f32[2,8]{1,0:T(2,128)S(1)}, f32[2,8]{1,0:T(2,128)}, u32[]{:S(2)}) %copy-start) | copy-done | bytes 88
  0.7 37.7 %lod_step.1 = f32[4,256,128]{2,1,0:T(8,128)S(1)} custom-call(f32[4,16,2048]{2,1,0:T(8,128)} %sal_hbm.1, s32[4,16,2048]{2,1,0:T(8,128)} %zone_hbm.1, f32[4,16,2048]{2,1,0:T(8,128)} %flow_hbm.1, s32[4,16,2048]{2,1,0:T(8,128)} %fixed_hbm.1, f32[2,8]{1,0:T(2,128)S(1)} %copy-done), custom_call_target="tpu_custom_call" | custom-call | tf_op jit(solution)/shard_map/lod_step/pallas_call | solution.py:619
  38.4 0.8 %copy.7 = f32[4,256,128]{2,1,0:T(8,128)} copy(f32[4,256,128]{2,1,0:T(8,128)S(1)} %lod_step.1) | data formatting | bytes 1048576
Async XLA Ops:
  0.0 0.7 %copy-start = (f32[2,8]{1,0:T(2,128)S(1)}, f32[2,8]{1,0:T(2,128)}, u32[]{:S(2)}) copy-start(f32[2,8]{1,0:T(2,128)} %disp_ref.1) | copy-start | bytes 196

commit v6 on v5

--- a/solution.py
+++ b/solution.py
@@ -57,6 +57,9 @@
     grp = lax.axis_index("grp")
     col = lax.axis_index("col")
     lay = lax.axis_index("lay")
+
+    def partner(m):
+        return ((col // 4 + (4 - m // 4) % 4) % 4) * 4 + (col % 4 + m % 4) % 4
 
     def s_copy(dest, source):
         return pltpu.make_async_remote_copy(
@@ -241,7 +244,7 @@
     pl.semaphore_wait(barrier, NCOL - 1 + NGRP - 1 + NLAY - 1)
 
     def s_start(o, carry):
-        s_copy((col + o) % NCOL, col).start()
+        s_copy(partner(o), col).start()
         return carry
 
     lax.fori_loop(1, NCOL, s_start, 0)
@@ -352,7 +355,7 @@
         ct[b, L : 2 * L] = q[L * b : L * (b + 1)]
 
     def c_start(o, carry):
-        c_copy((col + o) % NCOL, col).start()
+        c_copy(partner(o), col).start()
         return carry
 
     lax.fori_loop(1, NCOL, c_start, 0)
@@ -368,7 +371,7 @@
             ft_flat[pl.ds(8 * STEP * m + j, 8, stride=STEP), :] = x[8 * m : 8 * m + 8]
 
     def f_start(o, carry):
-        f_copy((col + o) % NCOL, col).start()
+        f_copy(partner(o), col).start()
         return carry
 
     lax.fori_loop(1, NCOL, f_start, 0)
@@ -417,8 +420,6 @@
     for o in range(1, NGRP):
         g_copy(gcoef, gc_send, gc_recv, (grp + o) % NGRP, grp).start()
 
-    e_stage(0)
-
     def c_wait(o, carry):
         c_copy(col, (col + NCOL - o) % NCOL).wait_recv()
         return carry
@@ -440,6 +441,8 @@
 
     for o in range(1, NGRP):
         g_copy(gval, gv_send, gv_recv, (grp + o) % NGRP, grp).start()
+
+    e_stage(0)
 
     to_left = jnp.zeros(whole, F32)
     to_right = jnp.ones(whole, F32)
@@ -499,13 +502,15 @@
     tmp[2] = f
     tmp[3] = jnp.where(block == RB - 1, right, pltpu.roll(f, LINES - 1, 0))
 
-    def f_wait(o, carry):
-        f_copy(col, (col + NCOL - o) % NCOL).wait_recv()
-        return carry
-
-    lax.fori_loop(1, NCOL, f_wait, 0)
 
     def fill(c):
+        for n in range(QR // RB):
+            source = c * (QR // RB) + n
+
+            @pl.when(source != col)
+            def _():
+                f_copy(col, source).wait_recv()
+
         for z in range(L):
             for n in range(QR // RB):
                 rows = pl.ds(pl.multiple_of(c * QR + RB * n, RB), RB)
@@ -517,7 +522,8 @@
         order = list(range(L) if way == 0 else range(L - 1, -1, -1))
         behind = k - 1 if way == 0 else k + 1
 
-        def step(c, carry):
+        def step(i, carry):
+            c = (i + col // 4) % QCH
             rows = pl.ds(pl.multiple_of(c * QR, QR), QR)
             if back < 2:
                 fill(c)
@@ -555,7 +561,8 @@
             below_from = {0: None, 1: 0, 2: 1, 3: 2}[k]
             above_from = {0: 1, 1: 2, 2: 3, 3: None}[k]
 
-            def finish(c, carry):
+            def finish(i, carry):
+                c = (i + col // 4) % QCH
                 rows = pl.ds(pl.multiple_of(c * QR, QR), QR)
                 if k in (0, NLAY - 1):
                     q_copy(0, c, k, 1 if k == 0 else 2).wait_recv()

time: 39.3 us -> 39 us (level)
  no operation moved by 1% of the time
where the time goes in v6:
time: 39 us; the launch traced here: 38.9 us
  Pallas kernels  37.4 us (96%)
  local copies, waits for them, and re-layouts  1.47 us (4%)
    pallas_call x1, Pallas kernels, per_device(): pl.pallas_call(kernel, out_shape=jax.ShapeDtypeStruct(slab, F32), in_spec...  37.4 us
    unnamed x3, local copies, waits for them, and re-layouts  1.47 us

profile of v6, /device:TPU:1, one launch (start us, length us, event | category | flops | bytes accessed | tf_op | source)
XLA Modules:
  0.0 38.9 jit_solution(2093596343545739981)
XLA Ops:
  0.0 0.0 copy-start
  0.0 0.7 %copy-done = f32[2,8]{1,0:T(2,128)S(1)} copy-done((f32[2,8]{1,0:T(2,128)S(1)}, f32[2,8]{1,0:T(2,128)}, u32[]{:S(2)}) %copy-start) | copy-done | bytes 88
  0.7 37.4 %lod_step.1 = f32[4,256,128]{2,1,0:T(8,128)S(1)} custom-call(f32[4,16,2048]{2,1,0:T(8,128)} %sal_hbm.1, s32[4,16,2048]{2,1,0:T(8,128)} %zone_hbm.1, f32[4,16,2048]{2,1,0:T(8,128)} %flow_hbm.1, s32[4,16,2048]{2,1,0:T(8,128)} %fixed_hbm.1, f32[2,8]{1,0:T(2,128)S(1)} %copy-done), custom_call_target="tpu_custom_call" | custom-call | tf_op jit(solution)/shard_map/lod_step/pallas_call | solution.py:626
  38.1 0.8 %copy.7 = f32[4,256,128]{2,1,0:T(8,128)} copy(f32[4,256,128]{2,1,0:T(8,128)S(1)} %lod_step.1) | data formatting | bytes 1048576
Async XLA Ops:
  0.0 0.7 %copy-start = (f32[2,8]{1,0:T(2,128)S(1)}, f32[2,8]{1,0:T(2,128)}, u32[]{:S(2)}) copy-start(f32[2,8]{1,0:T(2,128)} %disp_ref.1) | copy-start | bytes 196

commit v7 on v6

--- a/solution.py
+++ b/solution.py
@@ -172,7 +172,7 @@
             @pl.when(lay == (k if way == 0 else NLAY - 1 - k))
             def _():
                 me = k if way == 0 else NLAY - 1 - k
-                src, out, wr, pr, prod = ((eu_in, eu_out, wu, pu, ru), (ed_in, ed_out, wd, pd, rd))[way]
+                src, out, wr, pr = ((eu_in, eu_out, wu, pu), (ed_in, ed_out, wd, pd))[way]
 
                 def step(c, carry):
                     rows = pl.ds(pl.multiple_of(c * ZR, ZR), ZR)
@@ -181,7 +181,8 @@
                         e = src[rows, :]
                     else:
                         e = jnp.ones((ZR, LANES), F32)
-                    total = None
+                    if k == NLAY - 1 and way == 1:
+                        return carry
                     for i in range(L) if way == 0 else range(L - 1, -1, -1):
                         s = ys[i, rows, :]
                         se = s * e
@@ -190,9 +191,8 @@
                         p = s * w
                         wr[i, rows, :] = w
                         pr[i, rows, :] = p
-                        total = p if total is None else total * p
-                    out[rows, :] = e
-                    prod[rows, :] = total
+                    if k < NLAY - 1:
+                        out[rows, :] = e
                     if k < NLAY - 1:
                         e_copy(way, c, ahead(way, me)[0]).start()
                     return carry

time: 39 us -> 39 us (level)
  no operation moved by 1% of the time
where the time goes in v7:
time: 39 us; the launch traced here: 38.9 us
  Pallas kernels  37.4 us (96%)
  local copies, waits for them, and re-layouts  1.47 us (4%)
    pallas_call x1, Pallas kernels, per_device(): pl.pallas_call(kernel, out_shape=jax.ShapeDtypeStruct(slab, F32), in_spec...  37.4 us
    unnamed x3, local copies, waits for them, and re-layouts  1.47 us

profile of v7, /device:TPU:1, one launch (start us, length us, event | category | flops | bytes accessed | tf_op | source)
XLA Modules:
  0.0 38.9 jit_solution(13879569652989482675)
XLA Ops:
  0.0 0.0 copy-start
  0.0 0.7 %copy-done = f32[2,8]{1,0:T(2,128)S(1)} copy-done((f32[2,8]{1,0:T(2,128)S(1)}, f32[2,8]{1,0:T(2,128)}, u32[]{:S(2)}) %copy-start) | copy-done | bytes 88
  0.7 37.4 %lod_step.1 = f32[4,256,128]{2,1,0:T(8,128)S(1)} custom-call(f32[4,16,2048]{2,1,0:T(8,128)} %sal_hbm.1, s32[4,16,2048]{2,1,0:T(8,128)} %zone_hbm.1, f32[4,16,2048]{2,1,0:T(8,128)} %flow_hbm.1, s32[4,16,2048]{2,1,0:T(8,128)} %fixed_hbm.1, f32[2,8]{1,0:T(2,128)S(1)} %copy-done), custom_call_target="tpu_custom_call" | custom-call | tf_op jit(solution)/shard_map/lod_step/pallas_call | solution.py:626
  38.1 0.8 %copy.7 = f32[4,256,128]{2,1,0:T(8,128)} copy(f32[4,256,128]{2,1,0:T(8,128)S(1)} %lod_step.1) | data formatting | bytes 1048576
Async XLA Ops:
  0.0 0.7 %copy-start = (f32[2,8]{1,0:T(2,128)S(1)}, f32[2,8]{1,0:T(2,128)}, u32[]{:S(2)}) copy-start(f32[2,8]{1,0:T(2,128)} %disp_ref.1) | copy-start | bytes 196
